TPU v7x, 512 devices: a whole 4x4x16 slice. The times are simulated.
512 devices in a mesh: rep: 8 (over z_lo), blk: 64 (over y, z_hi, x, core).
Axes of the slice: x: 4, y: 4, z: 16 (z_hi: 2, z_lo: 8; z = z_hi * 8 + z_lo), core: 2. Of those that a mesh axis runs over, the one named last changes fastest.
Arguments:
- features: bfloat16 [65536, 256], P(('rep', 'blk')), may hold values from -6 to 6
- weight: bfloat16 [256, 256], replicated, may hold values from -0.375 to 0.375
- cotangent: bfloat16 [65536, 256], P(('rep', 'blk')), may hold values from -6 to 6
- tile_row: int32 [8, 64, 8, 4], P('rep', 'blk'), may hold values from 0 to 511, as said below
- tile_col: int32 [8, 64, 8, 4], P('rep', 'blk'), may hold values from 0 to 511, as said below
- tile_count: int32 [8, 64, 8], P('rep', 'blk'), may hold values from 1 to 4, as said below
- tile_vals: bfloat16 [8, 64, 8, 4, 128, 128], P('rep', 'blk'), may hold values from 0 to 0.015625
Outputs:
- activations: bfloat16 [65536, 256], P(('rep', 'blk'))
- weight_grad: float32 [256, 256], replicated
- feature_grad: bfloat16 [65536, 256], P(('rep', 'blk'))
Inputs may be any that keep to these rules, and one draw needn't show every extreme that they name: In slot (r, p, t, k) the row block lies in row panel p: p * 8 <= tile_row < (p + 1) * 8. The live slots of one (r, p, t) hold distinct (tile_row, tile_col) pairs. In slot (r, p, t, k) the column block lies in column panel q = (p - 8 * r - t) mod 64: q * 8 <= tile_col < (q + 1) * 8. Slots with k >= tile_count[r, p, t] are unused. `tile_count`: the value 4 occurs in every draw.
All inputs are finite; a program needn't handle non-finite values.
Results may differ from a plain program's by a relative error of at most 0.018.
Values may be sent and summed in bfloat16 or wider, within the bound.
A program may use at most 64 MiB of HBM per device.

v0:
```python
import math

import jax
import jax.numpy as jnp
from jax import lax
from jax.sharding import PartitionSpec as P


def passed_along(array, axis, by):
    peers = lax.axis_size(axis)
    return lax.ppermute(array, axis, [(i, (i + by) % peers) for i in range(peers)])


def silu_slope(values):
    sigmoid_part = jax.nn.sigmoid(values)
    return sigmoid_part * (1.0 + values * (1.0 - sigmoid_part))


def block_select(block_ids, live_slots, blocks):
    levels = lax.broadcasted_iota(jnp.int32, (block_ids.shape[0], blocks), 1)
    return ((block_ids[:, None] == levels) & live_slots[:, None]).astype(jnp.float32)


def forward_terms(panel, tiles, rows_local, cols_local, live_slots):
    picked = jnp.take(panel, cols_local, axis=0)
    product = jnp.einsum("kij,kjf->kif", tiles, picked, preferred_element_type=jnp.float32)
    select_rows = block_select(rows_local, live_slots, panel.shape[0])
    return jnp.einsum("kc,kif->cif", select_rows, product, precision=lax.Precision.HIGHEST)


def backward_terms(panel, tiles, rows_local, cols_local, live_slots):
    picked = jnp.take(panel, rows_local, axis=0)
    product = jnp.einsum("kji,kjf->kif", tiles, picked, preferred_element_type=jnp.float32)
    select_cols = block_select(cols_local, live_slots, panel.shape[0])
    return jnp.einsum("kc,kif->cif", select_cols, product, precision=lax.Precision.HIGHEST)


def on_device(features, weight, cotangent, tile_row, tile_col, tile_count, tile_vals):
    slab_rows, width = features.shape
    groups = lax.axis_size("rep")
    panels = lax.axis_size("blk")
    steps = panels // groups
    tile_size = tile_vals.shape[-1]
    blocks = groups * slab_rows // tile_size
    slots = tile_vals.shape[3]
    member = lax.axis_index("rep")
    rows_local = tile_row[0, 0] % blocks
    cols_local = tile_col[0, 0] % blocks
    live_slots = lax.broadcasted_iota(jnp.int32, (steps, slots), 1) < tile_count[0, 0][:, None]
    tiles = tile_vals[0, 0]
    total_nodes = slab_rows * groups * panels

    def forward_at(panel, index):
        return forward_terms(
            panel, tiles[index], rows_local[index], cols_local[index], live_slots[index]
        )

    def backward_at(panel, index):
        return backward_terms(
            panel, tiles[index], rows_local[index], cols_local[index], live_slots[index]
        )

    panel = lax.all_gather(features, "rep", axis=0, tiled=True)
    for level in range(groups.bit_length() - 1):
        moved = passed_along(panel, "blk", steps << level)
        panel = jnp.where(member >> level & 1 == 1, moved, panel)
    panel = panel.reshape(blocks, tile_size, width)
    partial_value = forward_at(panel, 0)
    for index in range(1, steps):
        panel = passed_along(panel, "blk", 1)
        partial_value = partial_value + forward_at(panel, index)
    row_part = lax.psum_scatter(
        partial_value.reshape(-1, width), "rep", scatter_dimension=0, tiled=True
    )
    aggregated = row_part.astype(jnp.bfloat16)
    preact = jnp.dot(aggregated, weight, preferred_element_type=jnp.float32)
    activations = jax.nn.silu(preact).astype(jnp.bfloat16)
    slope_grad = (cotangent.astype(jnp.float32) * silu_slope(preact)).astype(jnp.bfloat16)
    local_grad = jnp.dot(aggregated.T, slope_grad, preferred_element_type=jnp.float32)
    weight_grad = lax.psum(local_grad, ("rep", "blk")) * (1.0 / math.sqrt(total_nodes))
    back_rows = jnp.dot(slope_grad, weight.T, preferred_element_type=jnp.float32).astype(
        jnp.bfloat16
    )
    grad_panel = lax.all_gather(back_rows, "rep", axis=0, tiled=True).reshape(
        blocks, tile_size, width
    )
    carried = backward_at(grad_panel, steps - 1)
    for index in range(steps - 2, -1, -1):
        carried = passed_along(carried, "blk", -1) + backward_at(grad_panel, index)
    for level in range(groups.bit_length() - 1):
        moved = passed_along(carried.astype(jnp.bfloat16), "blk", -(steps << level)).astype(
            carried.dtype
        )
        carried = jnp.where(member >> level & 1 == 1, moved, carried)
    column_part = lax.psum_scatter(
        carried.reshape(-1, width).astype(jnp.bfloat16), "rep", scatter_dimension=0, tiled=True
    )
    return (activations, weight_grad, column_part)


def solution(mesh):
    return jax.shard_map(
        on_device,
        mesh=mesh,
        in_specs=(
            P(("rep", "blk"), None),
            P(),
            P(("rep", "blk"), None),
            P("rep", "blk", None, None),
            P("rep", "blk", None, None),
            P("rep", "blk", None),
            P("rep", "blk", None, None, None, None),
        ),
        out_specs=(P(("rep", "blk"), None), P(), P(("rep", "blk"), None)),
        check_vma=False,
    )
```

profile of v0, /device:TPU:1, one launch (start us, length us, event | category | flops | bytes accessed | tf_op | source)
XLA Modules:
  0.0 1381.1 jit_solution(2886629018027375451)
XLA Ops:
  7.2 46.8 %all_gather.6 = bf16[1024,256]{1,0:T(8,128)(2,1)S(1)} all-gather(bf16[128,256]{1,0:T(8,128)(2,1)} %param.9), channel_id=1, replica_groups=mesh['rep'=8,'blk'=64] {'rep'}, dimensions={0}, use_global_device_ids=true | all-gather | bytes 589824 | tf_op jit(solution)/shard_map/all_gather | solution.py:63
  54.0 11.7 collective-permute-start
  67.3 42.3 %collective-permute-done = bf16[1024,256]{1,0:T(8,128)(2,1)S(1)} collective-permute-done((bf16[1024,256]{1,0:T(8,128)(2,1)S(1)}, bf16[1024,256]{1,0:T(8,128)(2,1)S(1)}, u32[]{:S(2)}, u32[]{:S(2)}) %collective-permute-start) | collective-permute-done | bytes 524320 | tf_op jit(solution)/shard_map/ppermute | solution.py:11
  112.2 11.2 collective-permute-done.1
  161.9 14.8 %collective-permute-done.4 = bf16[8,128,256]{2,1,0:T(8,128)(2,1)} collective-permute-done((bf16[8,128,256]{2,1,0:T(8,128)(2,1)}, bf16[8,128,256]{2,1,0:T(8,128)(2,1)}, u32[]{:S(2)}, u32[]{:S(2)}) %collective-permute-start.4) | collective-permute-done | bytes 524320 | tf_op jit(solution)/shard_map/ppermute | solution.py:11
  182.6 20.9 %collective-permute-done.5 = bf16[8,128,256]{2,1,0:T(8,128)(2,1)} collective-permute-done((bf16[8,128,256]{2,1,0:T(8,128)(2,1)}, bf16[8,128,256]{2,1,0:T(8,128)(2,1)}, u32[]{:S(2)}, u32[]{:S(2)}) %collective-permute-start.5) | collective-permute-done | bytes 524320 | tf_op jit(solution)/shard_map/ppermute | solution.py:11
  210.1 21.1 %collective-permute-done.6 = bf16[8,128,256]{2,1,0:T(8,128)(2,1)} collective-permute-done((bf16[8,128,256]{2,1,0:T(8,128)(2,1)}, bf16[8,128,256]{2,1,0:T(8,128)(2,1)}, u32[]{:S(2)}, u32[]{:S(2)}) %collective-permute-start.6) | collective-permute-done | bytes 524320 | tf_op jit(solution)/shard_map/ppermute | solution.py:11
  237.8 20.3 %collective-permute-done.7 = bf16[8,128,256]{2,1,0:T(8,128)(2,1)} collective-permute-done((bf16[8,128,256]{2,1,0:T(8,128)(2,1)}, bf16[8,128,256]{2,1,0:T(8,128)(2,1)}, u32[]{:S(2)}, u32[]{:S(2)}) %collective-permute-start.7) | collective-permute-done | bytes 524320 | tf_op jit(solution)/shard_map/ppermute | solution.py:11
  264.7 21.1 %collective-permute-done.8 = bf16[8,128,256]{2,1,0:T(8,128)(2,1)} collective-permute-done((bf16[8,128,256]{2,1,0:T(8,128)(2,1)}, bf16[8,128,256]{2,1,0:T(8,128)(2,1)}, u32[]{:S(2)}, u32[]{:S(2)}) %collective-permute-start.8) | collective-permute-done | bytes 524320 | tf_op jit(solution)/shard_map/ppermute | solution.py:11
  292.3 20.3 %collective-permute-done.9 = bf16[8,128,256]{2,1,0:T(8,128)(2,1)} collective-permute-done((bf16[8,128,256]{2,1,0:T(8,128)(2,1)}, bf16[8,128,256]{2,1,0:T(8,128)(2,1)}, u32[]{:S(2)}, u32[]{:S(2)}) %collective-permute-start.9) | collective-permute-done | bytes 524320 | tf_op jit(solution)/shard_map/ppermute | solution.py:11
  318.0 72.7 %reduce-scatter.3.cloned.1.call-done = f32[128,256]{1,0:T(8,128)} async-done(((f32[1024,256]{1,0:T(8,128)}), f32[128,256]{1,0:T(8,128)}) %reduce-scatter.3.cloned.1.call-update) | async-done | bytes 131088 | tf_op jit(solution)/shard_map/reduce_scatter | solution.py:72
  392.6 42.6 %all_gather.7 = bf16[1024,256]{1,0:T(8,128)(2,1)S(1)} all-gather(bf16[128,256]{1,0:T(8,128)(2,1)S(1)} %convolution_convert_fusion), channel_id=1, replica_groups=mesh['rep'=8,'blk'=64] {'rep'}, dimensions={0}, use_global_device_ids=true | all-gather | bytes 589824 | tf_op jit(solution)/shard_map/all_gather | solution.py:84
  438.1 13.9 %collective-permute-start.10 = (f32[8,128,256]{2,0,1:T(8,128)}, f32[8,128,256]{2,0,1:T(8,128)}, u32[]{:S(2)}, u32[]{:S(2)}) collective-permute-start(f32[8,128,256]{2,0,1:T(8,128)} %fusion.14), channel_id=1, source_target_pairs={{0,63},{1,0},{2,1},{3,2},{4,3},{5,4},{6,5},{7,6},{8,7},{9,8},{10,9... | collective-permute-start | bytes 3145736 | tf_op jit(solution)/shard_map/ppermute | solution.py:11
  453.2 12.6 collective-permute-done.10
  468.8 29.3 %collective-permute-start.11 = (f32[8,128,256]{2,0,1:T(8,128)}, f32[8,128,256]{2,0,1:T(8,128)}, u32[]{:S(2)}, u32[]{:S(2)}) collective-permute-start(f32[8,128,256]{2,0,1:T(8,128)} %convolution_add_fusion), channel_id=1, source_target_pairs={{0,63},{1,0},{2,1},{3,2},{4,3},{5,4},{6,5},{7,6},{8,7},{9,8},{10,9... | collective-permute-start | bytes 3145736 | tf_op jit(solution)/shard_map/ppermute | solution.py:11
  503.2 35.1 %collective-permute-start.12 = (f32[8,128,256]{2,0,1:T(8,128)}, f32[8,128,256]{2,0,1:T(8,128)}, u32[]{:S(2)}, u32[]{:S(2)}) collective-permute-start(f32[8,128,256]{2,0,1:T(8,128)} %add.81), channel_id=1, source_target_pairs={{0,63},{1,0},{2,1},{3,2},{4,3},{5,4},{6,5},{7,6},{8,7},{9,8},{10,9... | collective-permute-start | bytes 3145736 | tf_op jit(solution)/shard_map/ppermute | solution.py:11
  543.3 36.0 %collective-permute-start.13 = (f32[8,128,256]{2,0,1:T(8,128)}, f32[8,128,256]{2,0,1:T(8,128)}, u32[]{:S(2)}, u32[]{:S(2)}) collective-permute-start(f32[8,128,256]{2,0,1:T(8,128)} %add.82), channel_id=1, source_target_pairs={{0,63},{1,0},{2,1},{3,2},{4,3},{5,4},{6,5},{7,6},{8,7},{9,8},{10,9... | collective-permute-start | bytes 3145736 | tf_op jit(solution)/shard_map/ppermute | solution.py:11
  584.4 46.6 %collective-permute-start.14 = (f32[8,128,256]{2,0,1:T(8,128)}, f32[8,128,256]{2,0,1:T(8,128)}, u32[]{:S(2)}, u32[]{:S(2)}) collective-permute-start(f32[8,128,256]{2,0,1:T(8,128)} %add.83), channel_id=1, source_target_pairs={{0,63},{1,0},{2,1},{3,2},{4,3},{5,4},{6,5},{7,6},{8,7},{9,8},{10,9... | collective-permute-start | bytes 3145736 | tf_op jit(solution)/shard_map/ppermute | solution.py:11
  636.0 42.8 %collective-permute-start.15 = (f32[8,128,256]{2,0,1:T(8,128)}, f32[8,128,256]{2,0,1:T(8,128)}, u32[]{:S(2)}, u32[]{:S(2)}) collective-permute-start(f32[8,128,256]{2,0,1:T(8,128)} %add.84), channel_id=1, source_target_pairs={{0,63},{1,0},{2,1},{3,2},{4,3},{5,4},{6,5},{7,6},{8,7},{9,8},{10,9... | collective-permute-start | bytes 3145736 | tf_op jit(solution)/shard_map/ppermute | solution.py:11
  682.9 46.6 %collective-permute-start.16 = (f32[8,128,256]{2,0,1:T(8,128)S(1)}, f32[8,128,256]{2,0,1:T(8,128)}, u32[]{:S(2)}, u32[]{:S(2)}) collective-permute-start(f32[8,128,256]{2,0,1:T(8,128)S(1)} %add.85), channel_id=1, source_target_pairs={{0,63},{1,0},{2,1},{3,2},{4,3},{5,4},{6,5},{7,6},{8,7},{9,8},{10,9... | collective-permute-start | bytes 3145736 | tf_op jit(solution)/shard_map/ppermute | solution.py:11
  733.2 9.2 collective-permute-start.17
  742.5 51.3 %collective-permute-done.17 = bf16[8,128,256]{2,0,1:T(8,128)(2,1)S(1)} collective-permute-done((bf16[8,128,256]{2,0,1:T(8,128)(2,1)S(1)}, bf16[8,128,256]{2,0,1:T(8,128)(2,1)S(1)}, u32[]{:S(2)}, u32[]{:S(2)}) %collective-permute-start.17) | collective-permute-done | bytes 524320 | tf_op jit(solution)/shard_map/ppermute | solution.py:11
  817.1 497.4 %all-reduce.2.cloned.1.call-done = f32[256,256]{1,0:T(8,128)} async-done(((f32[256,256]{1,0:T(8,128)}), f32[256,256]{1,0:T(8,128)}) %all-reduce.2.cloned.1.call-update) | async-done | bytes 262160 | tf_op jit(solution)/shard_map/psum | solution.py:80
  1316.2 58.4 %reduce-scatter.5.cloned.1.call-done = bf16[128,256]{1,0:T(8,128)(2,1)} async-done(((bf16[1024,256]{1,0:T(8,128)(2,1)}), bf16[128,256]{1,0:T(8,128)(2,1)}) %reduce-scatter.5.cloned.1.call-update) | async-done | bytes 65552 | tf_op jit(solution)/shard_map/reduce_scatter | solution.py:95
  (179 shorter events, 141.3 us)
Async XLA Ops:
  7.2 383.5 %copy-start = (bf16[256,256]{1,0:T(8,128)(2,1)S(1)}, bf16[256,256]{1,0:T(8,128)(2,1)}, u32[]{:S(2)}) copy-start(bf16[256,256]{1,0:T(8,128)(2,1)} %param.10) | copy-start | bytes 393220
  7.2 383.4 %reduce-scatter.3.cloned.1.call-start = ((), (), s32[]{:S(2)}) async-start(), calls=%async_computation.2 | async-start | bytes 1179648 | tf_op jit(solution)/shard_map/reduce_scatter | solution.py:72
  54.0 55.6 %collective-permute-start = (bf16[1024,256]{1,0:T(8,128)(2,1)S(1)}, bf16[1024,256]{1,0:T(8,128)(2,1)S(1)}, u32[]{:S(2)}, u32[]{:S(2)}) collective-permute-start(bf16[1024,256]{1,0:T(8,128)(2,1)S(1)} %all_gather.6), channel_id=1, source_target_pairs={{0,8},{1,9},{2,10},{3,11},{4,12},{5,13},{6,14},{7,15},{8,16},{9,17... | collective-permute-start | bytes 1572872 | tf_op jit(solution)/shard_map/ppermute | solution.py:11
  109.7 13.7 collective-permute-start.1
  123.4 13.9 %collective-permute-start.2 = (bf16[1024,256]{1,0:T(8,128)(2,1)S(1)}, bf16[1024,256]{1,0:T(8,128)(2,1)S(1)}, u32[]{:S(2)}, u32[]{:S(2)}) collective-permute-start(bf16[1024,256]{1,0:T(8,128)(2,1)S(1)} %broadcast_select_fusion.1), channel_id=1, source_target_pairs={{0,32},{1,33},{2,34},{3,35},{4,36},{5,37},{6,38},{7,39},{8,40},{9,... | collective-permute-start | bytes 1572872 | tf_op jit(solution)/shard_map/ppermute | solution.py:11
  138.2 14.5 %collective-permute-start.3 = (bf16[8,128,256]{2,1,0:T(8,128)(2,1)}, bf16[8,128,256]{2,1,0:T(8,128)(2,1)}, u32[]{:S(2)}, u32[]{:S(2)}) collective-permute-start(bf16[8,128,256]{2,1,0:T(8,128)(2,1)} %bitcast.5), channel_id=1, source_target_pairs={{0,1},{1,2},{2,3},{3,4},{4,5},{5,6},{6,7},{7,8},{8,9},{9,10},{10,1... | collective-permute-start | bytes 1572872 | tf_op jit(solution)/shard_map/ppermute | solution.py:11
  152.7 24.0 %collective-permute-start.4 = (bf16[8,128,256]{2,1,0:T(8,128)(2,1)}, bf16[8,128,256]{2,1,0:T(8,128)(2,1)}, u32[]{:S(2)}, u32[]{:S(2)}) collective-permute-start(bf16[8,128,256]{2,1,0:T(8,128)(2,1)} %collective-permute-done.3), channel_id=1, source_target_pairs={{0,1},{1,2},{2,3},{3,4},{4,5},{5,6},{6,7},{7,8},{8,9},{9,10},{10,1... | collective-permute-start | bytes 1572872 | tf_op jit(solution)/shard_map/ppermute | solution.py:11
  176.7 26.8 %collective-permute-start.5 = (bf16[8,128,256]{2,1,0:T(8,128)(2,1)}, bf16[8,128,256]{2,1,0:T(8,128)(2,1)}, u32[]{:S(2)}, u32[]{:S(2)}) collective-permute-start(bf16[8,128,256]{2,1,0:T(8,128)(2,1)} %collective-permute-done.4), channel_id=1, source_target_pairs={{0,1},{1,2},{2,3},{3,4},{4,5},{5,6},{6,7},{7,8},{8,9},{9,10},{10,1... | collective-permute-start | bytes 1572872 | tf_op jit(solution)/shard_map/ppermute | solution.py:11
  203.5 27.7 %collective-permute-start.6 = (bf16[8,128,256]{2,1,0:T(8,128)(2,1)}, bf16[8,128,256]{2,1,0:T(8,128)(2,1)}, u32[]{:S(2)}, u32[]{:S(2)}) collective-permute-start(bf16[8,128,256]{2,1,0:T(8,128)(2,1)} %collective-permute-done.5), channel_id=1, source_target_pairs={{0,1},{1,2},{2,3},{3,4},{4,5},{5,6},{6,7},{7,8},{8,9},{9,10},{10,1... | collective-permute-start | bytes 1572872 | tf_op jit(solution)/shard_map/ppermute | solution.py:11
  231.2 26.9 %collective-permute-start.7 = (bf16[8,128,256]{2,1,0:T(8,128)(2,1)}, bf16[8,128,256]{2,1,0:T(8,128)(2,1)}, u32[]{:S(2)}, u32[]{:S(2)}) collective-permute-start(bf16[8,128,256]{2,1,0:T(8,128)(2,1)} %collective-permute-done.6), channel_id=1, source_target_pairs={{0,1},{1,2},{2,3},{3,4},{4,5},{5,6},{6,7},{7,8},{8,9},{9,10},{10,1... | collective-permute-start | bytes 1572872 | tf_op jit(solution)/shard_map/ppermute | solution.py:11
  258.1 27.6 %collective-permute-start.8 = (bf16[8,128,256]{2,1,0:T(8,128)(2,1)}, bf16[8,128,256]{2,1,0:T(8,128)(2,1)}, u32[]{:S(2)}, u32[]{:S(2)}) collective-permute-start(bf16[8,128,256]{2,1,0:T(8,128)(2,1)} %collective-permute-done.7), channel_id=1, source_target_pairs={{0,1},{1,2},{2,3},{3,4},{4,5},{5,6},{6,7},{7,8},{8,9},{9,10},{10,1... | collective-permute-start | bytes 1572872 | tf_op jit(solution)/shard_map/ppermute | solution.py:11
  285.8 26.9 %collective-permute-start.9 = (bf16[8,128,256]{2,1,0:T(8,128)(2,1)}, bf16[8,128,256]{2,1,0:T(8,128)(2,1)}, u32[]{:S(2)}, u32[]{:S(2)}) collective-permute-start(bf16[8,128,256]{2,1,0:T(8,128)(2,1)} %collective-permute-done.8), channel_id=1, source_target_pairs={{0,1},{1,2},{2,3},{3,4},{4,5},{5,6},{6,7},{7,8},{8,9},{9,10},{10,1... | collective-permute-start | bytes 1572872 | tf_op jit(solution)/shard_map/ppermute | solution.py:11
  317.7 996.8 %all-reduce.2.cloned.1.call-start = ((), (), s32[]{:S(2)}) async-start(), calls=%async_computation.3 | async-start | bytes 524288 | tf_op jit(solution)/shard_map/psum | solution.py:80
  438.1 27.7 %collective-permute-start.10 = (f32[8,128,256]{2,0,1:T(8,128)}, f32[8,128,256]{2,0,1:T(8,128)}, u32[]{:S(2)}, u32[]{:S(2)}) collective-permute-start(f32[8,128,256]{2,0,1:T(8,128)} %fusion.14), channel_id=1, source_target_pairs={{0,63},{1,0},{2,1},{3,2},{4,3},{5,4},{6,5},{7,6},{8,7},{9,8},{10,9... | collective-permute-start | bytes 3145736 | tf_op jit(solution)/shard_map/ppermute | solution.py:11
  468.8 31.9 %collective-permute-start.11 = (f32[8,128,256]{2,0,1:T(8,128)}, f32[8,128,256]{2,0,1:T(8,128)}, u32[]{:S(2)}, u32[]{:S(2)}) collective-permute-start(f32[8,128,256]{2,0,1:T(8,128)} %convolution_add_fusion), channel_id=1, source_target_pairs={{0,63},{1,0},{2,1},{3,2},{4,3},{5,4},{6,5},{7,6},{8,7},{9,8},{10,9... | collective-permute-start | bytes 3145736 | tf_op jit(solution)/shard_map/ppermute | solution.py:11
  503.2 37.7 %collective-permute-start.12 = (f32[8,128,256]{2,0,1:T(8,128)}, f32[8,128,256]{2,0,1:T(8,128)}, u32[]{:S(2)}, u32[]{:S(2)}) collective-permute-start(f32[8,128,256]{2,0,1:T(8,128)} %add.81), channel_id=1, source_target_pairs={{0,63},{1,0},{2,1},{3,2},{4,3},{5,4},{6,5},{7,6},{8,7},{9,8},{10,9... | collective-permute-start | bytes 3145736 | tf_op jit(solution)/shard_map/ppermute | solution.py:11
  543.3 38.6 %collective-permute-start.13 = (f32[8,128,256]{2,0,1:T(8,128)}, f32[8,128,256]{2,0,1:T(8,128)}, u32[]{:S(2)}, u32[]{:S(2)}) collective-permute-start(f32[8,128,256]{2,0,1:T(8,128)} %add.82), channel_id=1, source_target_pairs={{0,63},{1,0},{2,1},{3,2},{4,3},{5,4},{6,5},{7,6},{8,7},{9,8},{10,9... | collective-permute-start | bytes 3145736 | tf_op jit(solution)/shard_map/ppermute | solution.py:11
  584.4 49.2 %collective-permute-start.14 = (f32[8,128,256]{2,0,1:T(8,128)}, f32[8,128,256]{2,0,1:T(8,128)}, u32[]{:S(2)}, u32[]{:S(2)}) collective-permute-start(f32[8,128,256]{2,0,1:T(8,128)} %add.83), channel_id=1, source_target_pairs={{0,63},{1,0},{2,1},{3,2},{4,3},{5,4},{6,5},{7,6},{8,7},{9,8},{10,9... | collective-permute-start | bytes 3145736 | tf_op jit(solution)/shard_map/ppermute | solution.py:11
  636.0 45.4 %collective-permute-start.15 = (f32[8,128,256]{2,0,1:T(8,128)}, f32[8,128,256]{2,0,1:T(8,128)}, u32[]{:S(2)}, u32[]{:S(2)}) collective-permute-start(f32[8,128,256]{2,0,1:T(8,128)} %add.84), channel_id=1, source_target_pairs={{0,63},{1,0},{2,1},{3,2},{4,3},{5,4},{6,5},{7,6},{8,7},{9,8},{10,9... | collective-permute-start | bytes 3145736 | tf_op jit(solution)/shard_map/ppermute | solution.py:11
  682.9 49.0 %collective-permute-start.16 = (f32[8,128,256]{2,0,1:T(8,128)S(1)}, f32[8,128,256]{2,0,1:T(8,128)}, u32[]{:S(2)}, u32[]{:S(2)}) collective-permute-start(f32[8,128,256]{2,0,1:T(8,128)S(1)} %add.85), channel_id=1, source_target_pairs={{0,63},{1,0},{2,1},{3,2},{4,3},{5,4},{6,5},{7,6},{8,7},{9,8},{10,9... | collective-permute-start | bytes 3145736 | tf_op jit(solution)/shard_map/ppermute | solution.py:11
  733.2 60.5 %collective-permute-start.17 = (bf16[8,128,256]{2,0,1:T(8,128)(2,1)S(1)}, bf16[8,128,256]{2,0,1:T(8,128)(2,1)S(1)}, u32[]{:S(2)}, u32[]{:S(2)}) collective-permute-start(bf16[8,128,256]{2,0,1:T(8,128)(2,1)S(1)} %add.86), channel_id=1, source_target_pairs={{0,56},{1,57},{2,58},{3,59},{4,60},{5,61},{6,62},{7,63},{8,0},{9,1... | collective-permute-start | bytes 1572872 | tf_op jit(solution)/shard_map/ppermute | solution.py:11
  793.9 10.1 collective-permute-start.18
  804.2 11.7 collective-permute-start.19
  809.2 565.4 %reduce-scatter.5.cloned.1.call-start = ((), (), s32[]{:S(2)}) async-start(), calls=%async_computation.4 | async-start | bytes 589824 | tf_op jit(solution)/shard_map/reduce_scatter | solution.py:95
  (11 other events, 173.8 us)
Sparse Core Ops, SparseCore 0:
  317.8 72.7 reduce-scatter.2
  809.3 505.1 all-reduce.1
  1318.1 56.4 reduce-scatter.4
where the time goes:
time: 1390 us; the launch traced here: 1380 us
  waiting for transfers between devices  893 us (64%)
  starting transfers between devices  308 us (22%)
  blocking collectives  89.4 us (6%)
  matrix products  30.3 us (2%)
  local copies, waits for them, and re-layouts  29.2 us (2%)
  other arithmetic  16.2 us (1%)
  between operations  14.8 us (1%)
    psum x1, waiting for transfers between devices, on_device(): lax.psum(local_grad, ('rep', 'blk')) * (1.0 / math.sqrt(total_nodes))  497 us
    ppermute x20, starting transfers between devices, passed_along(): lax.ppermute(array, axis, [(i, (i + by) % peers) for i in range(peers)])  308 us
    ppermute x20, waiting for transfers between devices, passed_along(): lax.ppermute(array, axis, [(i, (i + by) % peers) for i in range(peers)])  265 us
    reduce_scatter x1, waiting for transfers between devices, on_device(): lax.psum_scatter(partial_value.reshape(-1, width), 'rep', scatter_dimensi...  72.7 us
    reduce_scatter x1, waiting for transfers between devices, on_device(): lax.psum_scatter(carried.reshape(-1, width).astype(jnp.bfloat16), 'rep',...  58.4 us
    all_gather x1, blocking collectives, on_device(): panel = lax.all_gather(features, 'rep', axis=0, tiled=True)  46.8 us
    all_gather x1, blocking collectives, on_device(): lax.all_gather(back_rows, 'rep', axis=0, tiled=True)  42.6 us
  transfers between devices with their start and end apart: 23, of which 23 were waited for; matrix products, arithmetic and copies ran while one was open for 3% of the time, Pallas kernels for 0%

commit v1 on v0

v1 whole, which is shorter than its diff:
```python
import functools
import math

import jax
import jax.numpy as jnp
from jax import lax
from jax.experimental import pallas as pl
from jax.experimental.pallas import tpu as pltpu
from jax.sharding import PartitionSpec as P

BF16 = jnp.bfloat16
F32 = jnp.float32
MESH = pl.DeviceIdType.MESH


def layer_kernel(
    dims,
    feat_ref,
    weight_ref,
    cot_ref,
    row_ref,
    col_ref,
    count_ref,
    tile_ref,
    act_ref,
    wgrad_ref,
    fgrad_ref,
    zbuf,
    feats,
    lhs,
    rhs,
    acc,
    accb,
    rsin,
    gpanel,
    cbuf,
    sibin,
    xout,
    xin,
    yout,
    zpart,
    zin,
    zout,
    w_own,
    w_full,
    w_sib,
    w_half,
    w_xin,
    w_quart,
    w_yin,
    w_eight,
    w_zin,
    send,
    recv,
):
    R, X, Y, Z, S, K, B, nodes = dims
    r = lax.axis_index("rep")
    p = lax.axis_index("blk")
    c = p % 2
    x = (p // 2) % X
    zh = (p // S) % 2
    y = p // (2 * S)
    s = p % S
    z = zh * R + r

    def at(y_, z_, x_, c_):
        return {"rep": z_ % R, "blk": ((y_ * 2 + z_ // R) * X + x_) * 2 + c_}

    def z_dev(off):
        return at(y, (z + off + Z) % Z, x, c)

    def y_dev(off):
        return at((y + off) % Y, z, x, c)

    def x_dev(off):
        return at(y, z, (x + off) % X, c)

    sib = at(y, z, x, 1 - c)
    used = [0]

    def slots(n):
        used[0] += n
        return used[0] - n

    def copy(src, dst, i, dev):
        return pltpu.make_async_remote_copy(
            src_ref=src,
            dst_ref=dst,
            send_sem=send.at[i],
            recv_sem=recv.at[i],
            device_id=dev,
            device_id_type=MESH,
        )

    def arrived(dst, i):
        copy(dst, dst, i, sib).wait_recv()

    peers = [z_dev(d) for d in range(1, Z)] + [y_dev(d) for d in range(1, Y)]
    peers += [x_dev(d) for d in range(1, X)] + [sib]
    barrier = pltpu.get_barrier_semaphore()
    for dev in peers:
        pl.semaphore_signal(barrier, inc=1, device_id=dev, device_id_type=MESH)
    zbuf[z] = feat_ref[...]
    pl.semaphore_wait(barrier, len(peers))

    sent = []

    def go(cp):
        cp.start()
        sent.append(cp)

    def slot_of(n):
        return (z - (n + 1) // 2 + Z) % Z if n % 2 else (z + n // 2) % Z

    q = slots(Z)
    for n in range(Z):
        slot = slot_of(n)
        if n:
            arrived(zbuf.at[slot], q + n)
        for m in (1, 2) if n == 0 else (n + 2,):
            if m < Z:
                go(copy(zbuf.at[slot], zbuf.at[slot], q + m, z_dev(1 if m % 2 else -1)))

    q = slots(2)
    y_moves = []
    for half in range(2):
        e = (2 * y + half + r - zh + R) % R
        w = e % 2
        to = ((e + w) // 2) % Y
        src = zbuf.at[pl.ds(half * R, R)]
        dst = feats.at[s * (1 - w) + S * w]
        here = to == y

        @pl.when(here)
        def _():
            pltpu.make_async_copy(src, dst, recv.at[q + w]).start()

        @pl.when(jnp.logical_not(here))
        def _():
            copy(src, dst, q + w, at(to, z, x, c)).start()

        y_moves.append((src, dst, q + w, to))
    arrived(feats.at[s], q)
    arrived(feats.at[S], q + 1)
    for src, dst, i, to in y_moves:

        @pl.when(to != y)
        def _():
            copy(src, dst, i, sib).wait_send()

    q = slots(X)
    qs = slots(X)
    go(copy(feats.at[s * (1 - c) + S * c], feats.at[s], qs, sib))
    for d in range(1, X):
        xd = (x + d) % X
        later = (x < xd).astype(jnp.int32)
        go(copy(feats.at[s * later + S * (1 - later)], feats.at[s], q + d, x_dev(d)))
    for d in range(1, X):
        slot = feats.at[2 * ((x - d + X) % X) + c]
        arrived(slot, q + d)
        go(copy(slot, slot, qs + d, sib))
    for d in range(X):
        arrived(feats.at[2 * ((x - d + X) % X) + 1 - c], qs + d)

    acc[...] = jnp.zeros_like(acc)

    def forward_step(t, _):
        panel = (s - t + S) % S
        for k in range(K):
            rhs[k * B : (k + 1) * B, :] = feats[panel, col_ref[t, k] % R]
            row = row_ref[t, k] % R
            live = k < count_ref[t]
            tile = tile_ref[t * K + k]
            for b in range(R):
                keep = jnp.logical_and(live, row == b)
                lhs[b * B : (b + 1) * B, k * B : (k + 1) * B] = jnp.where(
                    keep, tile, jnp.zeros_like(tile)
                )
        for b in range(R):
            rows = slice(b * B, (b + 1) * B)
            acc[rows, :] += jnp.dot(lhs[rows, :], rhs[...], preferred_element_type=F32)
        return 0

    lax.fori_loop(0, S, forward_step, 0)

    q = slots(R)
    for d in range(1, R):
        rd = (r + d) % R
        accb[d] = acc[pl.ds(pl.multiple_of(rd * B, B), B), :].astype(BF16)
        go(copy(accb.at[d], rsin.at[d], q + d, at(y, zh * R + rd, x, c)))
    total = acc[pl.ds(pl.multiple_of(r * B, B), B), :]
    for d in range(1, R):
        arrived(rsin.at[d], q + d)
        total = total + rsin[d].astype(F32)

    agg = total.astype(BF16)
    preact = jnp.dot(agg, weight_ref[...], preferred_element_type=F32)
    sig = 1.0 / (1.0 + jnp.exp(-preact))
    act_ref[...] = (preact * sig).astype(BF16)
    slope = (cot_ref[...].astype(F32) * (sig * (1.0 + preact * (1.0 - sig)))).astype(BF16)
    back = lax.dot_general(
        slope, weight_ref[...], (((1,), (1,)), ((), ())), preferred_element_type=F32
    )
    gpanel[r] = back.astype(BF16)
    q = slots(R)
    for d in range(1, R):
        rd = (r + d) % R
        go(copy(gpanel.at[r], gpanel.at[r], q + d, at(y, zh * R + rd, x, c)))
    w_own[...] = lax.dot_general(
        agg, slope, (((0,), (0,)), ((), ())), preferred_element_type=F32
    )
    half_rows = w_half.shape[0]
    x_rows = w_quart.shape[0]
    y_rows = w_eight.shape[0]

    def w_rows(i, n):
        return pl.ds(pl.multiple_of(i * n, n), n)

    qw = slots(1)
    go(copy(w_own.at[w_rows(1 - c, half_rows)], w_sib, qw, sib))
    for d in range(1, R):
        arrived(gpanel.at[(r - d + R) % R], q + d)
    arrived(w_sib, qw)
    w_half[...] = w_own[w_rows(c, half_rows), :] + w_sib[...]
    qw = slots(X)
    for d in range(1, X):
        xd = (x + d) % X
        go(copy(w_half.at[w_rows(xd, x_rows)], w_xin.at[x], qw + d, x_dev(d)))
    w_xin[x] = w_half[w_rows(x, x_rows), :]

    def backward_step(t, _):
        panel = (s - t + S) % S
        for k in range(K):
            rhs[k * B : (k + 1) * B, :] = gpanel[row_ref[t, k] % R]
            col = col_ref[t, k] % R
            live = k < count_ref[t]
            tile = tile_ref[t * K + k].T
            for b in range(R):
                keep = jnp.logical_and(live, col == b)
                lhs[b * B : (b + 1) * B, k * B : (k + 1) * B] = jnp.where(
                    keep, tile, jnp.zeros_like(tile)
                )
        for b in range(R):
            rows = slice(b * B, (b + 1) * B)
            cbuf[panel, b] = jnp.dot(
                lhs[rows, :], rhs[...], preferred_element_type=F32
            ).astype(BF16)
        return 0

    lax.fori_loop(0, S, backward_step, 0)

    qs = slots(X)
    for d in list(range(1, X)) + [0]:
        go(copy(cbuf.at[2 * ((x + d) % X) + 1 - c], sibin.at[d], qs + d, sib))

    for d in range(1, X):
        arrived(w_xin.at[(x - d + X) % X], qw + d)
    w_quart[...] = functools.reduce(lambda a, b: a + b, [w_xin[i] for i in range(X)])
    qw = slots(Y)
    for d in range(1, Y):
        yd = (y + d) % Y
        go(copy(w_quart.at[w_rows(yd, y_rows)], w_yin.at[y], qw + d, y_dev(d)))
    w_yin[y] = w_quart[w_rows(y, y_rows), :]

    q = slots(X)
    for d in range(1, X):
        arrived(sibin.at[d], qs + d)
        for b in range(R):
            xout[d, b] = (
                cbuf[2 * ((x + d) % X) + c, b].astype(F32) + sibin[d, b].astype(F32)
            ).astype(BF16)
        go(copy(xout.at[d], xin.at[d], q + d, x_dev(d)))

    for d in range(1, Y):
        arrived(w_yin.at[(y - d + Y) % Y], qw + d)
    w_eight[...] = functools.reduce(lambda a, b: a + b, [w_yin[i] for i in range(Y)])
    w_zin[z] = w_eight[...]
    qw = slots(Z)
    for d in range(1, Z):
        go(copy(w_eight, w_zin.at[z], qw + d, z_dev(d)))

    arrived(sibin.at[0], qs)
    for d in range(1, X):
        arrived(xin.at[d], q + d)
    for b in range(R):
        mine = sibin[0, b].astype(F32)
        first = cbuf[s, b].astype(F32) + jnp.where(c == 0, mine, 0.0)
        second = jnp.where(c == 1, mine, 0.0)
        for d in range(1, X):
            part = xin[d, b].astype(F32)
            above = (x - d + X) % X > x
            first = first + jnp.where(above, part, 0.0)
            second = second + jnp.where(above, 0.0, part)
        yout[0, b] = first.astype(BF16)
        yout[1, b] = second.astype(BF16)

    q = slots(2)
    y_moves = []
    for w in range(2):
        panel = (2 * y + zh - r - w + 2 * R) % R
        to, half = panel // 2, panel % 2
        dst = zpart.at[pl.ds(half * R, R)]

        @pl.when(to == y)
        def _():
            pltpu.make_async_copy(yout.at[w], dst, recv.at[q + half]).start()

        @pl.when(to != y)
        def _():
            copy(yout.at[w], dst, q + half, at(to, z, x, c)).start()

        y_moves.append((yout.at[w], dst, q + half, to))

    for d in range(1, Z):
        arrived(w_zin.at[(z - d + Z) % Z], qw + d)
    out_row = c * half_rows + x * x_rows + y * y_rows
    scale = 1.0 / math.sqrt(nodes)
    wgrad_rows = pl.ds(pl.multiple_of(out_row, y_rows), y_rows)
    w_full[wgrad_rows, :] = (
        functools.reduce(lambda a, b: a + b, [w_zin[i] for i in range(Z)]) * scale
    )
    qw = slots(Y)
    for d in range(1, Y):
        go(copy(w_full.at[wgrad_rows], w_full.at[wgrad_rows], qw + d, y_dev(d)))

    for half in range(2):
        arrived(zpart.at[pl.ds(half * R, R)], q + half)

    def w_piece(c_, x_, y_):
        at_row = c_ * half_rows + x_ * x_rows
        if y_ is None:
            return w_full.at[pl.ds(pl.multiple_of(at_row, x_rows), x_rows)]
        at_row = at_row + y_ * y_rows
        return w_full.at[pl.ds(pl.multiple_of(at_row, y_rows), y_rows)]

    for d in range(1, Y):
        arrived(w_piece(c, x, (y - d + Y) % Y), qw + d)
    qw = slots(X)
    piece = w_piece(c, x, None)
    for d in range(1, X):
        go(copy(piece, piece, qw + d, x_dev(d)))

    q = slots(Z)

    def z_step(n):
        slot = slot_of(n)
        src = zpart.at[slot]
        if n + 2 < Z:
            arrived(zin.at[n], q + n)
            zout[n] = (zpart[slot].astype(F32) + zin[n].astype(F32)).astype(BF16)
            src = zout.at[n]
        land = n - 2 if n >= 2 else Z - 1
        go(copy(src, zin.at[land], q + land, z_dev(-1 if n % 2 else 1)))

    for n in range(Z - 1, Z // 2 - 1, -1):
        z_step(n)
    for d in range(1, X):
        arrived(w_piece(c, (x - d + X) % X, None), qw + d)
    qw = slots(1)
    rows = w_full.at[w_rows(c, half_rows)]
    go(copy(rows, rows, qw, sib))
    for n in range(Z // 2 - 1, 0, -1):
        z_step(n)
    arrived(zin.at[Z - 1], q + Z - 1)
    arrived(zin.at[0], q)
    fgrad_ref[...] = (
        zpart[z].astype(F32) + zin[Z - 1].astype(F32) + zin[0].astype(F32)
    ).astype(BF16)
    arrived(w_full.at[w_rows(1 - c, half_rows)], qw)
    wgrad_ref[...] = w_full[...]

    for src, dst, i, to in y_moves:

        @pl.when(to != y)
        def _():
            copy(src, dst, i, sib).wait_send()

    for cp in sent:
        cp.wait_send()


def on_device(features, weight, cotangent, tile_row, tile_col, tile_count, tile_vals):
    B, F = features.shape
    R = lax.axis_size("rep")
    S = lax.axis_size("blk") // R
    K = tile_vals.shape[3]
    X, Y, Z = S // 2, R // 2, 2 * R
    nodes = B * R * R * S
    dims = (R, X, Y, Z, S, K, B, nodes)
    block = (B, F)
    vmem = pltpu.VMEM
    sems = 3 * Z + 2 + 2 + 6 * X + 2 * R + 2 * Y + 8
    scratch = [
        vmem((Z,) + block, BF16),
        vmem((S + 1, R) + block, BF16),
        vmem((R * B, K * B), BF16),
        vmem((K * B, F), BF16),
        vmem((R * B, F), F32),
        vmem((R,) + block, BF16),
        vmem((R,) + block, BF16),
        vmem((R,) + block, BF16),
        vmem((S, R) + block, BF16),
        vmem((X, R) + block, BF16),
        vmem((X, R) + block, BF16),
        vmem((X, R) + block, BF16),
        vmem((2, R) + block, BF16),
        vmem((Z,) + block, BF16),
        vmem((Z,) + block, BF16),
        vmem((Z,) + block, BF16),
        vmem((F, F), F32),
        vmem((F, F), F32),
        vmem((F // 2, F), F32),
        vmem((F // 2, F), F32),
        vmem((X, F // 2 // X, F), F32),
        vmem((F // 2 // X, F), F32),
        vmem((Y, F // 2 // X // Y, F), F32),
        vmem((F // 2 // X // Y, F), F32),
        vmem((Z, F // 2 // X // Y, F), F32),
        pltpu.SemaphoreType.DMA((sems,)),
        pltpu.SemaphoreType.DMA((sems,)),
    ]
    in_vmem = pl.BlockSpec(memory_space=pltpu.VMEM)
    in_smem = pl.BlockSpec(memory_space=pltpu.SMEM)
    return pl.pallas_call(
        functools.partial(layer_kernel, dims),
        out_shape=(
            jax.ShapeDtypeStruct(block, BF16),
            jax.ShapeDtypeStruct((F, F), F32),
            jax.ShapeDtypeStruct(block, BF16),
        ),
        in_specs=[in_vmem, in_vmem, in_vmem, in_smem, in_smem, in_smem, in_vmem],
        out_specs=(in_vmem, in_vmem, in_vmem),
        scratch_shapes=scratch,
        compiler_params=pltpu.CompilerParams(
            collective_id=0, has_side_effects=True, vmem_limit_bytes=48 << 20
        ),
        name="layer",
    )(
        features,
        weight,
        cotangent,
        tile_row[0, 0],
        tile_col[0, 0],
        tile_count[0, 0],
        tile_vals.reshape((S * K, B, B)),
    )


def solution(mesh):
    return jax.shard_map(
        on_device,
        mesh=mesh,
        in_specs=(
            P(("rep", "blk"), None),
            P(),
            P(("rep", "blk"), None),
            P("rep", "blk", None, None),
            P("rep", "blk", None, None),
            P("rep", "blk", None),
            P("rep", "blk", None, None, None, None),
        ),
        out_specs=(P(("rep", "blk"), None), P(), P(("rep", "blk"), None)),
        check_vma=False,
    )
```

time: 1390 us -> 227 us (0.16)
  the two profiles are of different devices: /device:TPU:1 before, /device:TPU:32 now
where the time goes in v1:
time: 227 us
  Pallas kernels  218 us (96%)
  local copies, waits for them, and re-layouts  7.78 us (3%)
    pallas_call x1, Pallas kernels, on_device(): pl.pallas_call(functools.partial(layer_kernel, dims), out_shape=(jax.Shap...  218 us
    unnamed x17, local copies, waits for them, and re-layouts  7.62 us

profile of v1, /device:TPU:32, one launch (start us, length us, event | category | flops | bytes accessed | tf_op | source)
XLA Modules:
  0.0 226.9 jit_solution(605225661414632557)
XLA Ops:
  0.6 0.0 copy-start.5
  0.6 0.7 copy-done.5
  1.3 0.0 copy-start.6
  1.3 0.1 copy.10.row_ref
  1.4 0.6 copy-done.6
  2.0 0.0 copy-start.4
  2.0 0.1 copy.11.col_ref
  2.1 0.6 copy-done.4
  2.7 0.0 copy-start
  2.7 1.2 copy-done
  3.9 0.0 copy-start.1
  3.9 0.9 copy-done.1
  4.8 0.0 copy-start.2
  4.8 0.8 copy-done.2
  5.6 0.0 copy-start.3
  5.6 0.8 copy-done.3
  6.5 218.4 %layer.1 = (bf16[128,256]{1,0:T(8,128)(2,1)S(1)}, f32[256,256]{1,0:T(8,128)S(1)}, bf16[128,256]{1,0:T(8,128)(2,1)S(1)}) custom-call(bf16[128,256]{1,0:T(8,128)(2,1)S(1)} %copy-done.2, bf16[256,256]{1,0:T(8,128)(2,1)S(1)} %copy-done.1, bf16[128,256]{1,0:T(8,128)(2,1)S(1)} %copy-done.3, s32[8,4]{1,0:T(8,128)S(1)} %copy.10.row_ref, s32[8,4]{1,0:T(8,128)S(1)} %copy.11.col_ref, ...), custom_call_target="tpu_custom_call" | custom-call | tf_op jit(solution)/shard_map/layer/pallas_call | solution.py:424
  224.9 0.6 copy.15
  225.5 0.7 copy.16
  226.2 0.6 copy.17
Async XLA Ops:
  0.6 0.7 copy-start.5
  1.3 0.7 copy-start.6
  2.0 0.7 copy-start.4
  2.7 1.2 copy-start
  3.9 0.9 copy-start.1
  4.8 0.8 copy-start.2
  5.6 0.8 copy-start.3

commit v2 on v1

v2 whole, which is shorter than its diff:
```python
import functools
import math

import jax
import jax.numpy as jnp
from jax import lax
from jax.experimental import pallas as pl
from jax.experimental.pallas import tpu as pltpu
from jax.sharding import PartitionSpec as P

BF16 = jnp.bfloat16
F32 = jnp.float32
MESH = pl.DeviceIdType.MESH


def layer_kernel(
    dims,
    feat_hbm,
    weight_hbm,
    cot_hbm,
    row_hbm,
    col_hbm,
    count_hbm,
    tile_hbm,
    act_ref,
    wgrad_ref,
    fgrad_ref,
    zbuf,
    feats,
    lhs,
    rhs,
    acc,
    accb,
    rsin,
    gpanel,
    cbuf,
    sibin,
    xout,
    xin,
    yout,
    zpart,
    zin,
    zout,
    w_own,
    w_full,
    w_sib,
    w_half,
    w_xin,
    w_quart,
    w_yin,
    w_eight,
    w_zin,
    weight_ref,
    cot_ref,
    row_ref,
    col_ref,
    count_ref,
    tile_ref,
    ysum,
    send,
    recv,
    load,
):
    R, X, Y, Z, S, K, B, nodes = dims
    r = lax.axis_index("rep")
    p = lax.axis_index("blk")
    c = p % 2
    x = (p // 2) % X
    zh = (p // S) % 2
    y = p // (2 * S)
    s = p % S
    z = zh * R + r

    def at(y_, z_, x_, c_):
        return {"rep": z_ % R, "blk": ((y_ * 2 + z_ // R) * X + x_) * 2 + c_}

    def z_dev(off):
        return at(y, (z + off + Z) % Z, x, c)

    def y_dev(off):
        return at((y + off) % Y, z, x, c)

    def x_dev(off):
        return at(y, z, (x + off) % X, c)

    sib = at(y, z, x, 1 - c)
    used = [0]

    def slots(n):
        used[0] += n
        return used[0] - n

    def copy(src, dst, i, dev):
        return pltpu.make_async_remote_copy(
            src_ref=src,
            dst_ref=dst,
            send_sem=send.at[i],
            recv_sem=recv.at[i],
            device_id=dev,
            device_id_type=MESH,
        )

    def arrived(dst, i):
        copy(dst, dst, i, sib).wait_recv()

    loads = [
        pltpu.make_async_copy(src, dst, load.at[i])
        for i, (src, dst) in enumerate(
            [
                (feat_hbm, zbuf.at[z]),
                (row_hbm, row_ref),
                (col_hbm, col_ref),
                (count_hbm, count_ref),
                (tile_hbm, tile_ref),
                (weight_hbm, weight_ref),
                (cot_hbm, cot_ref),
            ]
        )
    ]
    for cp in loads:
        cp.start()

    near = sorted({d % Z for d in (1, 2, -1, -2)} - {0})
    peers = [z_dev(d) for d in near] + [y_dev(d) for d in range(1, Y)]
    peers += [x_dev(d) for d in range(1, X)] + [sib]
    barrier = pltpu.get_barrier_semaphore()
    for dev in peers:
        pl.semaphore_signal(barrier, inc=1, device_id=dev, device_id_type=MESH)
    loads[0].wait()
    pl.semaphore_wait(barrier, len(peers))

    sent = []

    def go(cp):
        cp.start()
        sent.append(cp)

    up, down = Z // 2, Z - 1 - Z // 2
    levels = [[(1, 0)]]
    for top in range(2, up + 2, 2):
        level = [(g, m) for m in (top, top - 1) for g in (1, -1)]
        levels.append([(g, m) for g, m in level if m <= (up if g > 0 else down)])
    order = [e for level in levels for e in level]
    number = {e: n for n, e in enumerate(order)}

    def slot_of(e):
        return (z - e[0] * e[1] + Z) % Z

    def children(e):
        g, m = e
        if m % 2:
            return []
        both = [(1, 1), (-1, 1), (1, 2), (-1, 2)] if m == 0 else [(g, m + 1), (g, m + 2)]
        return [k for k in both if k in number]

    def role_of(e):
        return (zh + r + slot_of(e) // R) % 2

    qz, qy, qx, qs = slots(Z), slots(Z), slots(X * R), slots(X)

    def f_gather(e):
        slot = slot_of(e)
        if e[1]:
            arrived(zbuf.at[slot], qz + number[e])
        for k in children(e)[::-1]:
            hop = k[0] * (k[1] - e[1])
            go(copy(zbuf.at[slot], zbuf.at[slot], qz + number[k], z_dev(hop)))

    def f_y_to(e):
        return ((2 * y + slot_of(e) // R + role_of(e) + r - zh + R) % R) // 2

    def f_y_block(e):
        w = role_of(e)
        return feats.at[s * (1 - w) + S * w, slot_of(e) % R]

    def f_y(e):
        slot, to, i = slot_of(e), f_y_to(e), qy + number[e]

        @pl.when(to == y)
        def _():
            pltpu.make_async_copy(zbuf.at[slot], f_y_block(e), recv.at[i]).start()

        @pl.when(to != y)
        def _():
            copy(zbuf.at[slot], f_y_block(e), i, at(to, z, x, c)).start()

    def f_y_sent(e):
        @pl.when(f_y_to(e) != y)
        def _():
            copy(zbuf.at[slot_of(e)], f_y_block(e), qy + number[e], sib).wait_send()

    def f_x(e):
        w, b = role_of(e), slot_of(e) % R
        src = f_y_block(e)
        arrived(src, qy + number[e])
        for d in range(1, X):

            @pl.when((x < (x + d) % X) == (w == 0))
            def _():
                copy(src, feats.at[s, b], qx + d * R + b, x_dev(d)).start()

        @pl.when(w == c)
        def _():
            shared(src, feats.at[s, b], qs, sib).start()

    def f_core(e):
        w, b = role_of(e), slot_of(e) % R
        for d in range(1, X):
            xs = (x - d + X) % X

            @pl.when((xs < x) == (w == 0))
            def _():
                block = feats.at[2 * xs + c, b]
                arrived(block, qx + d * R + b)
                shared(block, block, qs + d, sib).start()

    def shared(src, dst, i, dev):
        return copy(src, dst, i, dev)

    for n in range(len(levels) + 2):
        if n < len(levels):
            for e in levels[n]:
                f_gather(e)
            for e in levels[n]:
                f_y(e)
        if 0 <= n - 1 < len(levels):
            for e in levels[n - 1]:
                f_x(e)
        if 0 <= n - 2:
            for e in levels[n - 2]:
                f_core(e)
    for d in range(X):
        arrived(feats.at[2 * ((x - d + X) % X) + 1 - c], qs + d)
    for d in range(X):
        copy(feats.at[s], feats.at[s], qs + d, sib).wait_send()
    for d in range(1, X):
        for b in range(R):
            copy(feats.at[s, b], feats.at[s, b], qx + d * R + b, sib).wait_send()
    for e in order:
        f_y_sent(e)
    for cp in loads[1:]:
        cp.wait()

    acc[...] = jnp.zeros_like(acc)

    def forward_step(t, _):
        panel = (s - t + S) % S
        for k in range(K):
            rhs[k * B : (k + 1) * B, :] = feats[panel, col_ref[k, t] % R]
            row = row_ref[k, t] % R
            live = k < count_ref[t]
            tile = tile_ref[t * K + k]
            for b in range(R):
                keep = jnp.logical_and(live, row == b)
                lhs[b * B : (b + 1) * B, k * B : (k + 1) * B] = jnp.where(
                    keep, tile, jnp.zeros_like(tile)
                )
        for b in range(R):
            rows = slice(b * B, (b + 1) * B)
            acc[rows, :] += jnp.dot(lhs[rows, :], rhs[...], preferred_element_type=F32)
        return 0

    lax.fori_loop(0, S, forward_step, 0)

    q = slots(R)
    for d in range(1, R):
        rd = (r + d) % R
        accb[d] = acc[pl.ds(pl.multiple_of(rd * B, B), B), :].astype(BF16)
        go(copy(accb.at[d], rsin.at[d], q + d, at(y, zh * R + rd, x, c)))
    total = acc[pl.ds(pl.multiple_of(r * B, B), B), :]
    for d in range(1, R):
        arrived(rsin.at[d], q + d)
        total = total + rsin[d].astype(F32)

    agg = total.astype(BF16)
    preact = jnp.dot(agg, weight_ref[...], preferred_element_type=F32)
    sig = 1.0 / (1.0 + jnp.exp(-preact))
    slope = (cot_ref[...].astype(F32) * (sig * (1.0 + preact * (1.0 - sig)))).astype(BF16)
    back = lax.dot_general(
        slope, weight_ref[...], (((1,), (1,)), ((), ())), preferred_element_type=F32
    )
    gpanel[r] = back.astype(BF16)
    q = slots(R)
    for d in range(1, R):
        rd = (r + d) % R
        go(copy(gpanel.at[r], gpanel.at[r], q + d, at(y, zh * R + rd, x, c)))
    act_ref[...] = (preact * sig).astype(BF16)
    w_own[...] = lax.dot_general(
        agg, slope, (((0,), (0,)), ((), ())), preferred_element_type=F32
    )
    half_rows = w_half.shape[0]
    x_rows = w_quart.shape[0]
    y_rows = w_eight.shape[0]

    def w_rows(i, n):
        return pl.ds(pl.multiple_of(i * n, n), n)

    qw = slots(1)
    go(copy(w_own.at[w_rows(1 - c, half_rows)], w_sib, qw, sib))
    for d in range(1, R):
        arrived(gpanel.at[(r - d + R) % R], q + d)
    arrived(w_sib, qw)
    w_half[...] = w_own[w_rows(c, half_rows), :] + w_sib[...]
    qw = slots(X)
    for d in range(1, X):
        xd = (x + d) % X
        go(copy(w_half.at[w_rows(xd, x_rows)], w_xin.at[x], qw + d, x_dev(d)))
    w_xin[x] = w_half[w_rows(x, x_rows), :]

    def backward_step(t, _):
        panel = (s - t + S) % S
        for k in range(K):
            rhs[k * B : (k + 1) * B, :] = gpanel[row_ref[k, t] % R]
            col = col_ref[k, t] % R
            live = k < count_ref[t]
            tile = tile_ref[t * K + k].T
            for b in range(R):
                keep = jnp.logical_and(live, col == b)
                lhs[b * B : (b + 1) * B, k * B : (k + 1) * B] = jnp.where(
                    keep, tile, jnp.zeros_like(tile)
                )
        for b in range(R):
            rows = slice(b * B, (b + 1) * B)
            cbuf[panel, b] = jnp.dot(
                lhs[rows, :], rhs[...], preferred_element_type=F32
            ).astype(BF16)

        @pl.when(panel % 2 != c)
        def _():
            d = (panel // 2 - x + X) % X
            copy(cbuf.at[panel], sibin.at[d], qs + d, sib).start()

        return 0

    qs = slots(X)
    lax.fori_loop(0, S, backward_step, 0)

    qx, qy, qz = slots(X * R), slots(Z), slots(Z)

    def b_x(e):
        w, b = role_of(e), slot_of(e) % R
        for d in range(1, X):
            xd = (x + d) % X

            @pl.when((xd < x) == (w == 0))
            def _():
                xout[d, b] = (
                    cbuf[2 * xd + c, b].astype(F32) + sibin[d, b].astype(F32)
                ).astype(BF16)
                copy(xout.at[d, b], xin.at[d, b], qx + d * R + b, x_dev(d)).start()

    def b_y_to(e):
        return ((2 * y + zh - r - role_of(e) + 2 * R) % R) // 2

    def b_y(e):
        w, b, i = role_of(e), slot_of(e) % R, qy + number[e]
        own = cbuf[s, b].astype(F32)
        other = sibin[0, b].astype(F32)
        ysum[...] = jnp.where(w == 0, own, 0.0) + jnp.where(w == c, other, 0.0)
        for d in range(1, X):

            @pl.when(((x - d + X) % X > x) == (w == 0))
            def _():
                arrived(xin.at[d, b], qx + d * R + b)
                ysum[...] += xin[d, b].astype(F32)

        src = yout.at[number[e]]
        src[...] = ysum[...].astype(BF16)
        dst, to = zpart.at[slot_of(e)], b_y_to(e)

        @pl.when(to == y)
        def _():
            pltpu.make_async_copy(src, dst, recv.at[i]).start()

        @pl.when(to != y)
        def _():
            copy(src, dst, i, at(to, z, x, c)).start()

    def b_y_sent(e):
        @pl.when(b_y_to(e) != y)
        def _():
            copy(yout.at[0], yout.at[0], qy + number[e], sib).wait_send()

    def b_z(e):
        g, m = e
        slot, n = slot_of(e), number[e]
        arrived(zpart.at[slot], qy + n)
        val = zpart[slot].astype(F32)
        for k in children(e):
            arrived(zin.at[number[k]], qz + number[k])
            val = val + zin[number[k]].astype(F32)
        if m == 0:
            fgrad_ref[...] = val.astype(BF16)
        else:
            zout[n] = val.astype(BF16)
            go(copy(zout.at[n], zin.at[n], qz + n, z_dev(-g * (2 - m % 2))))

    def w_piece(c_, x_, y_):
        at_row = c_ * half_rows + x_ * x_rows
        if y_ is None:
            return w_full.at[pl.ds(pl.multiple_of(at_row, x_rows), x_rows)]
        at_row = at_row + y_ * y_rows
        return w_full.at[pl.ds(pl.multiple_of(at_row, y_rows), y_rows)]

    def w_1():
        for d in range(1, X):
            arrived(w_xin.at[(x - d + X) % X], qw + d)
        w_quart[...] = functools.reduce(lambda a, b: a + b, [w_xin[i] for i in range(X)])
        i = slots(Y)
        for d in range(1, Y):
            yd = (y + d) % Y
            go(copy(w_quart.at[w_rows(yd, y_rows)], w_yin.at[y], i + d, y_dev(d)))
        w_yin[y] = w_quart[w_rows(y, y_rows), :]
        return i

    def w_2(i):
        for d in range(1, Y):
            arrived(w_yin.at[(y - d + Y) % Y], i + d)
        w_eight[...] = functools.reduce(lambda a, b: a + b, [w_yin[i] for i in range(Y)])
        w_zin[z] = w_eight[...]
        i = slots(Z)
        for d in range(1, Z):
            go(copy(w_eight, w_zin.at[z], i + d, z_dev(d)))
        return i

    def w_3(i):
        for d in range(1, Z):
            arrived(w_zin.at[(z - d + Z) % Z], i + d)
        piece = w_piece(c, x, y)
        piece[...] = functools.reduce(
            lambda a, b: a + b, [w_zin[i] for i in range(Z)]
        ) * (1.0 / math.sqrt(nodes))
        i = slots(Y)
        for d in range(1, Y):
            go(copy(piece, piece, i + d, y_dev(d)))
        return i

    def w_4(i):
        for d in range(1, Y):
            arrived(w_piece(c, x, (y - d + Y) % Y), i + d)
        piece = w_piece(c, x, None)
        i = slots(X)
        for d in range(1, X):
            go(copy(piece, piece, i + d, x_dev(d)))
        return i

    def w_5(i):
        for d in range(1, X):
            arrived(w_piece(c, (x - d + X) % X, None), i + d)
        rows = w_full.at[w_rows(c, half_rows)]
        i = slots(1)
        go(copy(rows, rows, i, sib))
        return i

    for d in range(X):
        arrived(sibin.at[d], qs + d)
    back_levels = levels[::-1]
    w_state = w_1()
    w_rest = [w_2, w_3, w_4, w_5]
    for n in range(len(levels) + 2):
        if n < len(levels):
            for e in back_levels[n]:
                b_x(e)
        if 0 <= n - 1 < len(levels):
            for e in back_levels[n - 1]:
                b_y(e)
        if 0 <= n - 2:
            for e in back_levels[n - 2]:
                b_z(e)
        if n >= 1 and w_rest:
            w_state = w_rest.pop(0)(w_state)
    while w_rest:
        w_state = w_rest.pop(0)(w_state)
    arrived(w_full.at[w_rows(1 - c, half_rows)], w_state)
    wgrad_ref[...] = w_full[...]

    for d in range(X):
        copy(cbuf.at[0], cbuf.at[0], qs + d, sib).wait_send()
    for d in range(1, X):
        for b in range(R):
            copy(xout.at[d, b], xout.at[d, b], qx + d * R + b, sib).wait_send()
    for e in order:
        b_y_sent(e)
    for cp in sent:
        cp.wait_send()


def on_device(features, weight, cotangent, tile_row, tile_col, tile_count, tile_vals):
    B, F = features.shape
    R = lax.axis_size("rep")
    S = lax.axis_size("blk") // R
    K = tile_vals.shape[3]
    X, Y, Z = S // 2, R // 2, 2 * R
    nodes = B * R * R * S
    dims = (R, X, Y, Z, S, K, B, nodes)
    block = (B, F)
    vmem = pltpu.VMEM
    sems = 5 * Z + 2 * X * R + 4 * X + 2 * R + 2 * Y + 8
    scratch = [
        vmem((Z,) + block, BF16),
        vmem((S + 1, R) + block, BF16),
        vmem((R * B, K * B), BF16),
        vmem((K * B, F), BF16),
        vmem((R * B, F), F32),
        vmem((R,) + block, BF16),
        vmem((R,) + block, BF16),
        vmem((R,) + block, BF16),
        vmem((S, R) + block, BF16),
        vmem((X, R) + block, BF16),
        vmem((X, R) + block, BF16),
        vmem((X, R) + block, BF16),
        vmem((Z,) + block, BF16),
        vmem((Z,) + block, BF16),
        vmem((Z,) + block, BF16),
        vmem((Z,) + block, BF16),
        vmem((F, F), F32),
        vmem((F, F), F32),
        vmem((F // 2, F), F32),
        vmem((F // 2, F), F32),
        vmem((X, F // 2 // X, F), F32),
        vmem((F // 2 // X, F), F32),
        vmem((Y, F // 2 // X // Y, F), F32),
        vmem((F // 2 // X // Y, F), F32),
        vmem((Z, F // 2 // X // Y, F), F32),
        vmem((F, F), BF16),
        vmem(block, BF16),
        pltpu.SMEM((K, S), jnp.int32),
        pltpu.SMEM((K, S), jnp.int32),
        pltpu.SMEM((S,), jnp.int32),
        vmem((S * K, B, B), BF16),
        vmem(block, F32),
        pltpu.SemaphoreType.DMA((sems,)),
        pltpu.SemaphoreType.DMA((sems,)),
        pltpu.SemaphoreType.DMA((7,)),
    ]
    in_vmem = pl.BlockSpec(memory_space=pltpu.VMEM)
    in_hbm = pl.BlockSpec(memory_space=pltpu.HBM)
    return pl.pallas_call(
        functools.partial(layer_kernel, dims),
        out_shape=(
            jax.ShapeDtypeStruct(block, BF16),
            jax.ShapeDtypeStruct((F, F), F32),
            jax.ShapeDtypeStruct(block, BF16),
        ),
        in_specs=[in_hbm] * 7,
        out_specs=(in_vmem, in_vmem, in_vmem),
        scratch_shapes=scratch,
        compiler_params=pltpu.CompilerParams(
            collective_id=0, has_side_effects=True, vmem_limit_bytes=63 << 20
        ),
        name="layer",
    )(
        features,
        weight,
        cotangent,
        tile_row[0, 0].T,
        tile_col[0, 0].T,
        tile_count[0, 0],
        tile_vals.reshape((S * K, B, B)),
    )


def solution(mesh):
    return jax.shard_map(
        on_device,
        mesh=mesh,
        in_specs=(
            P(("rep", "blk"), None),
            P(),
            P(("rep", "blk"), None),
            P("rep", "blk", None, None),
            P("rep", "blk", None, None),
            P("rep", "blk", None),
            P("rep", "blk", None, None, None, None),
        ),
        out_specs=(P(("rep", "blk"), None), P(), P(("rep", "blk"), None)),
        check_vma=False,
    )
```

time: 227 us -> 175 us (0.77)
  the two profiles are of different devices: /device:TPU:32 before, /device:TPU:1 now
where the time goes in v2:
time: 175 us; the launch traced here: 173 us
  Pallas kernels  168 us (96%)
  local copies, waits for them, and re-layouts  3.81 us (2%)
    pallas_call x1, Pallas kernels, on_device(): pl.pallas_call(functools.partial(layer_kernel, dims), out_shape=(jax.Shap...  168 us
    unnamed x5, local copies, waits for them, and re-layouts  3.81 us

profile of v2, /device:TPU:1, one launch (start us, length us, event | category | flops | bytes accessed | tf_op | source)
XLA Modules:
  0.0 172.6 jit_solution(17358871146151807591)
XLA Ops:
  0.6 168.2 %layer.1 = (bf16[128,256]{1,0:T(8,128)(2,1)}, f32[256,256]{1,0:T(8,128)}, bf16[128,256]{1,0:T(8,128)(2,1)}) custom-call(bf16[128,256]{1,0:T(8,128)(2,1)} %feat_hbm.1, bf16[256,256]{1,0:T(8,128)(2,1)} %weight_hbm.1, bf16[128,256]{1,0:T(8,128)(2,1)} %cot_hbm.1, s32[4,8]{1,0:T(4,128)} %bitcast.9, s32[4,8]{1,0:T(4,128)} %bitcast.10, s32[8]{0:T(128)} %bitcast.11, ...), custom_call_target="tpu_custom_call" | custom-call | tf_op jit(solution)/shard_map/layer/pallas_call | solution.py:538
  168.8 1.5 copy.13
  170.3 0.0 copy-start
  170.3 1.7 copy.14
  172.0 0.0 copy-done
  172.0 0.6 copy.15
Async XLA Ops:
  170.3 1.7 copy-start

commit v3 on v2

v3 whole, which is shorter than its diff:
```python
import functools
import math

import jax
import jax.numpy as jnp
from jax import lax
from jax.experimental import pallas as pl
from jax.experimental.pallas import tpu as pltpu
from jax.sharding import PartitionSpec as P

BF16 = jnp.bfloat16
LATE = 2.5
BLATE = 2.5
F32 = jnp.float32
MESH = pl.DeviceIdType.MESH


def layer_kernel(
    dims,
    feat_hbm,
    weight_hbm,
    cot_hbm,
    row_hbm,
    col_hbm,
    count_hbm,
    tile_hbm,
    act_ref,
    wgrad_ref,
    fgrad_ref,
    zbuf,
    feats_0,
    feats_1,
    lhs,
    rhs,
    acc,
    accb,
    rsin,
    rsown,
    agg_ref,
    gpanel_0,
    gpanel_1,
    cbuf,
    sibin,
    xout,
    xin,
    yout,
    zpart,
    zin,
    zout,
    w_own,
    w_full,
    w_sib,
    w_half,
    w_xin,
    w_quart,
    w_yin,
    w_eight,
    w_zin,
    weight_ref,
    cot_ref,
    row_ref,
    col_ref,
    count_ref,
    tile_ref,
    ysum,
    send,
    recv,
    load,
):
    R, X, Y, Z, S, K, B, HF, nodes = dims
    feats, gpanel = (feats_0, feats_1), (gpanel_0, gpanel_1)
    r = lax.axis_index("rep")
    p = lax.axis_index("blk")
    c = p % 2
    x = (p // 2) % X
    zh = (p // S) % 2
    y = p // (2 * S)
    s = p % S
    z = zh * R + r

    def at(y_, z_, x_, c_):
        return {"rep": z_ % R, "blk": ((y_ * 2 + z_ // R) * X + x_) * 2 + c_}

    def z_dev(off):
        return at(y, (z + off + Z) % Z, x, c)

    def y_dev(off):
        return at((y + off) % Y, z, x, c)

    def x_dev(off):
        return at(y, z, (x + off) % X, c)

    sib = at(y, z, x, 1 - c)
    used = [0]

    def slots(n):
        used[0] += n
        return used[0] - n

    def copy(src, dst, i, dev):
        return pltpu.make_async_remote_copy(
            src_ref=src,
            dst_ref=dst,
            send_sem=send.at[i],
            recv_sem=recv.at[i],
            device_id=dev,
            device_id_type=MESH,
        )

    def arrived(dst, i):
        copy(dst, dst, i, sib).wait_recv()

    def half_cols(h):
        return pl.ds(h * HF, HF)

    loads = [
        pltpu.make_async_copy(src, dst, load.at[i])
        for i, (src, dst) in enumerate(
            [
                (feat_hbm.at[:, half_cols(0)], zbuf.at[0, z]),
                (feat_hbm.at[:, half_cols(1)], zbuf.at[1, z]),
                (row_hbm, row_ref),
                (col_hbm, col_ref),
                (count_hbm, count_ref),
                (tile_hbm, tile_ref),
                (weight_hbm, weight_ref),
                (cot_hbm, cot_ref),
            ]
        )
    ]
    for cp in loads:
        cp.start()

    near = sorted({d % Z for d in (1, 2, -1, -2)} - {0})
    peers = [z_dev(d) for d in near] + [y_dev(d) for d in range(1, Y)]
    peers += [x_dev(d) for d in range(1, X)] + [sib]
    barrier = pltpu.get_barrier_semaphore()
    for dev in peers:
        pl.semaphore_signal(barrier, inc=1, device_id=dev, device_id_type=MESH)
    loads[0].wait()
    loads[1].wait()
    pl.semaphore_wait(barrier, len(peers))

    sent = []

    def go(cp):
        cp.start()
        sent.append(cp)

    up, down = Z // 2, Z - 1 - Z // 2
    levels = [[(1, 0)]]
    for top in range(2, up + 2, 2):
        level = [(g, m) for m in (top, top - 1) for g in (1, -1)]
        levels.append([(g, m) for g, m in level if m <= (up if g > 0 else down)])
    order = [e for level in levels for e in level]
    number = {e: n for n, e in enumerate(order)}

    def slot_of(e):
        return (z - e[0] * e[1] + Z) % Z

    def children(e):
        g, m = e
        if m % 2:
            return []
        both = [(1, 1), (-1, 1), (1, 2), (-1, 2)] if m == 0 else [(g, m + 1), (g, m + 2)]
        return [k for k in both if k in number]

    def role_of(e):
        return (zh + r + slot_of(e) // R) % 2

    fq = [(slots(Z), slots(Z), slots(X * R), slots(X)) for _ in range(2)]

    def f_gather(h, e):
        slot, qz = slot_of(e), fq[h][0]
        block = zbuf.at[h, slot]
        if e[1]:
            arrived(block, qz + number[e])
        for k in children(e)[::-1]:
            hop = k[0] * (k[1] - e[1])
            go(copy(block, block, qz + number[k], z_dev(hop)))

    def f_y_to(e):
        return ((2 * y + slot_of(e) // R + role_of(e) + r - zh + R) % R) // 2

    def f_y_block(h, e):
        w = role_of(e)
        return feats[h].at[s * (1 - w) + S * w, slot_of(e) % R]

    def f_y(h, e):
        slot, to, i = slot_of(e), f_y_to(e), fq[h][1] + number[e]

        @pl.when(to == y)
        def _():
            pltpu.make_async_copy(
                zbuf.at[h, slot], f_y_block(h, e), recv.at[i]
            ).start()

        @pl.when(to != y)
        def _():
            copy(zbuf.at[h, slot], f_y_block(h, e), i, at(to, z, x, c)).start()

    def f_y_sent(h, e):
        @pl.when(f_y_to(e) != y)
        def _():
            copy(zbuf.at[h, 0], zbuf.at[h, 0], fq[h][1] + number[e], sib).wait_send()

    def f_x(h, e):
        w, b = role_of(e), slot_of(e) % R
        src = f_y_block(h, e)
        _, qy, qx, qs = fq[h]
        arrived(src, qy + number[e])
        for d in range(1, X):

            @pl.when((x < (x + d) % X) == (w == 0))
            def _():
                copy(src, feats[h].at[s, b], qx + d * R + b, x_dev(d)).start()

        @pl.when(w == c)
        def _():
            copy(src, feats[h].at[s, b], qs, sib).start()

    def f_core(h, e):
        w, b = role_of(e), slot_of(e) % R
        _, _, qx, qs = fq[h]
        for d in range(1, X):
            xs = (x - d + X) % X

            @pl.when((xs < x) == (w == 0))
            def _():
                block = feats[h].at[2 * xs + c, b]
                arrived(block, qx + d * R + b)
                copy(block, block, qs + d, sib).start()

    def masked_tiles(ids, turned):
        def step(t, _):
            for k in range(K):
                live = k < count_ref[t]
                block = ids[k, t] % R
                tile = tile_ref[t * K + k]
                if turned:
                    tile = tile.T
                for b in range(R):
                    keep = jnp.logical_and(live, block == b)
                    lhs[t, b * B : (b + 1) * B, k * B : (k + 1) * B] = jnp.where(
                        keep, tile, jnp.zeros_like(tile)
                    )
            return 0

        lax.fori_loop(0, S, step, 0)

    def forward_products(h):
        acc[...] = jnp.zeros_like(acc)

        def step(t, _):
            panel = (s - t + S) % S
            for k in range(K):
                rhs[k * B : (k + 1) * B, :] = feats[h][panel, col_ref[k, t] % R]
            for b in range(R):
                rows = slice(b * B, (b + 1) * B)
                acc[rows, :] += jnp.dot(
                    lhs[t, rows, :], rhs[...], preferred_element_type=F32
                )
            return 0

        lax.fori_loop(0, S, step, 0)

    rq = [slots(R), slots(R)]
    own_rows = pl.ds(pl.multiple_of(r * B, B), B)

    def f_finish(h):
        qs = fq[h][3]
        for d in range(X):
            arrived(feats[h].at[2 * ((x - d + X) % X) + 1 - c], qs + d)
        forward_products(h)
        for d in range(1, R):
            rd = (r + d) % R
            accb[h, d] = acc[pl.ds(pl.multiple_of(rd * B, B), B), :].astype(BF16)
            go(copy(accb.at[h, d], rsin.at[h, d], rq[h] + d, at(y, zh * R + rd, x, c)))
        rsown[h] = acc[own_rows, :]

    def f_sent(h):
        _, _, qx, qs = fq[h]
        for d in range(X):
            copy(feats[h].at[0], feats[h].at[0], qs + d, sib).wait_send()
        for d in range(1, X):
            for b in range(R):
                copy(
                    feats[h].at[0, b], feats[h].at[0, b], qx + d * R + b, sib
                ).wait_send()
        for e in order:
            f_y_sent(h, e)

    events = []
    top = len(levels)
    for h in range(2):
        for n in range(top):
            late = n + LATE * h
            events += [(late, 0, "gather", h, n), (late + 1, 1, "x", h, n)]
            events += [(late + 2, 2, "core", h, n)]
        events += [(top + 1.1 + LATE * h, 3, "finish", h, 0)]
    events += [(2.5, 4, "tiles", 0, 0)]
    for _, _, what, h, n in sorted(events):
        if what == "gather":
            for e in levels[n]:
                f_gather(h, e)
            for e in levels[n]:
                f_y(h, e)
        elif what == "x":
            for e in levels[n]:
                f_x(h, e)
        elif what == "core":
            for e in levels[n]:
                f_core(h, e)
        elif what == "tiles":
            for cp in loads[2:]:
                cp.wait()
            masked_tiles(row_ref, False)
        else:
            f_finish(h)
    for h in range(2):
        total = rsown[h]
        for d in range(1, R):
            arrived(rsin.at[h, d], rq[h] + d)
            total = total + rsin[h, d].astype(F32)
        agg_ref[:, h * HF : (h + 1) * HF] = total.astype(BF16)

    agg = agg_ref[...]
    preact = jnp.dot(agg, weight_ref[...], preferred_element_type=F32)
    sig = 1.0 / (1.0 + jnp.exp(-preact))
    slope = (cot_ref[...].astype(F32) * (sig * (1.0 + preact * (1.0 - sig)))).astype(BF16)
    back = lax.dot_general(
        slope, weight_ref[...], (((1,), (1,)), ((), ())), preferred_element_type=F32
    )
    gq = [slots(R), slots(R)]
    for h in range(2):
        gpanel[h][r] = back[:, h * HF : (h + 1) * HF].astype(BF16)
        for d in range(1, R):
            rd = (r + d) % R
            mine = gpanel[h].at[r]
            go(copy(mine, mine, gq[h] + d, at(y, zh * R + rd, x, c)))
    act_ref[...] = (preact * sig).astype(BF16)
    w_own[...] = lax.dot_general(
        agg, slope, (((0,), (0,)), ((), ())), preferred_element_type=F32
    )
    half_rows = w_half.shape[0]
    x_rows = w_quart.shape[0]
    y_rows = w_eight.shape[0]

    def w_rows(i, n):
        return pl.ds(pl.multiple_of(i * n, n), n)

    qw = slots(1)
    go(copy(w_own.at[w_rows(1 - c, half_rows)], w_sib, qw, sib))
    masked_tiles(col_ref, True)
    arrived(w_sib, qw)
    w_half[...] = w_own[w_rows(c, half_rows), :] + w_sib[...]
    qw = slots(X)
    for d in range(1, X):
        xd = (x + d) % X
        go(copy(w_half.at[w_rows(xd, x_rows)], w_xin.at[x], qw + d, x_dev(d)))
    w_xin[x] = w_half[w_rows(x, x_rows), :]

    bq = [(slots(X), slots(X * R), slots(Z), slots(Z)) for _ in range(2)]

    def backward_products(h):
        for d in range(1, R):
            arrived(gpanel[h].at[(r - d + R) % R], gq[h] + d)

        def step(t, _):
            panel = (s - t + S) % S
            for k in range(K):
                rhs[k * B : (k + 1) * B, :] = gpanel[h][row_ref[k, t] % R]
            for b in range(R):
                rows = slice(b * B, (b + 1) * B)
                cbuf[h, panel, b] = jnp.dot(
                    lhs[t, rows, :], rhs[...], preferred_element_type=F32
                ).astype(BF16)

            @pl.when(panel % 2 != c)
            def _():
                d = (panel // 2 - x + X) % X
                copy(cbuf.at[h, panel], sibin.at[h, d], bq[h][0] + d, sib).start()

            return 0

        lax.fori_loop(0, S, step, 0)

    def b_x(h, e):
        w, b = role_of(e), slot_of(e) % R
        for d in range(1, X):
            xd = (x + d) % X

            @pl.when((xd < x) == (w == 0))
            def _():
                xout[h, d, b] = (
                    cbuf[h, 2 * xd + c, b].astype(F32) + sibin[h, d, b].astype(F32)
                ).astype(BF16)
                i = bq[h][1] + d * R + b
                copy(xout.at[h, d, b], xin.at[h, d, b], i, x_dev(d)).start()

    def b_y_to(e):
        return ((2 * y + zh - r - role_of(e) + 2 * R) % R) // 2

    def b_y(h, e):
        w, b, i = role_of(e), slot_of(e) % R, bq[h][2] + number[e]
        own = cbuf[h, s, b].astype(F32)
        other = sibin[h, 0, b].astype(F32)
        ysum[...] = jnp.where(w == 0, own, 0.0) + jnp.where(w == c, other, 0.0)
        for d in range(1, X):

            @pl.when(((x - d + X) % X > x) == (w == 0))
            def _():
                arrived(xin.at[h, d, b], bq[h][1] + d * R + b)
                ysum[...] += xin[h, d, b].astype(F32)

        src = yout.at[h, number[e]]
        src[...] = ysum[...].astype(BF16)
        dst, to = zpart.at[h, slot_of(e)], b_y_to(e)

        @pl.when(to == y)
        def _():
            pltpu.make_async_copy(src, dst, recv.at[i]).start()

        @pl.when(to != y)
        def _():
            copy(src, dst, i, at(to, z, x, c)).start()

    def b_y_sent(h, e):
        @pl.when(b_y_to(e) != y)
        def _():
            copy(yout.at[h, 0], yout.at[h, 0], bq[h][2] + number[e], sib).wait_send()

    def b_z(h, e):
        g, m = e
        slot, n, qz = slot_of(e), number[e], bq[h][3]
        arrived(zpart.at[h, slot], bq[h][2] + n)
        val = zpart[h, slot].astype(F32)
        for k in children(e):
            arrived(zin.at[h, number[k]], qz + number[k])
            val = val + zin[h, number[k]].astype(F32)
        if m == 0:
            fgrad_ref[:, h * HF : (h + 1) * HF] = val.astype(BF16)
        else:
            zout[h, n] = val.astype(BF16)
            go(copy(zout.at[h, n], zin.at[h, n], qz + n, z_dev(-g * (2 - m % 2))))

    def w_piece(c_, x_, y_):
        at_row = c_ * half_rows + x_ * x_rows
        if y_ is None:
            return w_full.at[pl.ds(pl.multiple_of(at_row, x_rows), x_rows)]
        at_row = at_row + y_ * y_rows
        return w_full.at[pl.ds(pl.multiple_of(at_row, y_rows), y_rows)]

    def w_1():
        for d in range(1, X):
            arrived(w_xin.at[(x - d + X) % X], qw + d)
        w_quart[...] = functools.reduce(lambda a, b: a + b, [w_xin[i] for i in range(X)])
        i = slots(Y)
        for d in range(1, Y):
            yd = (y + d) % Y
            go(copy(w_quart.at[w_rows(yd, y_rows)], w_yin.at[y], i + d, y_dev(d)))
        w_yin[y] = w_quart[w_rows(y, y_rows), :]
        return i

    def w_2(i):
        for d in range(1, Y):
            arrived(w_yin.at[(y - d + Y) % Y], i + d)
        w_eight[...] = functools.reduce(lambda a, b: a + b, [w_yin[i] for i in range(Y)])
        w_zin[z] = w_eight[...]
        i = slots(Z)
        for d in range(1, Z):
            go(copy(w_eight, w_zin.at[z], i + d, z_dev(d)))
        return i

    def w_3(i):
        for d in range(1, Z):
            arrived(w_zin.at[(z - d + Z) % Z], i + d)
        piece = w_piece(c, x, y)
        piece[...] = functools.reduce(
            lambda a, b: a + b, [w_zin[i] for i in range(Z)]
        ) * (1.0 / math.sqrt(nodes))
        i = slots(Y)
        for d in range(1, Y):
            go(copy(piece, piece, i + d, y_dev(d)))
        return i

    def w_4(i):
        for d in range(1, Y):
            arrived(w_piece(c, x, (y - d + Y) % Y), i + d)
        piece = w_piece(c, x, None)
        i = slots(X)
        for d in range(1, X):
            go(copy(piece, piece, i + d, x_dev(d)))
        return i

    def w_5(i):
        for d in range(1, X):
            arrived(w_piece(c, (x - d + X) % X, None), i + d)
        rows = w_full.at[w_rows(c, half_rows)]
        i = slots(1)
        go(copy(rows, rows, i, sib))
        return i

    back_levels = levels[::-1]
    for h in range(2):
        backward_products(h)
        if h == 0:
            w_state = w_1()
        for d in range(X):
            arrived(sibin.at[h, d], bq[h][0] + d)
        for level in back_levels:
            for e in level:
                b_x(h, e)
    events = []
    for h in range(2):
        for n in range(top):
            late = n + BLATE * h
            events += [(late, 0, "y", h, n), (late + 2, 1, "z", h, n)]
    w_rest = [w_2, w_3, w_4, w_5]
    events += [(1.5 + n * 1.5, 2, "w", 0, n) for n in range(len(w_rest))]
    for _, _, what, h, n in sorted(events):
        if what == "w":
            w_state = w_rest[n](w_state)
        else:
            for e in back_levels[n]:
                (b_y if what == "y" else b_z)(h, e)
    arrived(w_full.at[w_rows(1 - c, half_rows)], w_state)
    wgrad_ref[...] = w_full[...]

    for h in range(2):
        f_sent(h)
        qs, qx, _, _ = bq[h]
        for d in range(X):
            copy(cbuf.at[h, 0], cbuf.at[h, 0], qs + d, sib).wait_send()
        for d in range(1, X):
            for b in range(R):
                copy(
                    xout.at[h, d, b], xout.at[h, d, b], qx + d * R + b, sib
                ).wait_send()
        for e in order:
            b_y_sent(h, e)
    for cp in sent:
        cp.wait_send()


def on_device(features, weight, cotangent, tile_row, tile_col, tile_count, tile_vals):
    B, F = features.shape
    R = lax.axis_size("rep")
    S = lax.axis_size("blk") // R
    K = tile_vals.shape[3]
    X, Y, Z = S // 2, R // 2, 2 * R
    nodes = B * R * R * S
    HF = F // 2
    dims = (R, X, Y, Z, S, K, B, HF, nodes)
    block = (B, F)
    part = (B, HF)
    vmem = pltpu.VMEM
    sems = 9 * Z + 4 * X * R + 8 * X + 4 * R + 2 * Y + 8
    scratch = [
        vmem((2, Z) + part, BF16),
        vmem((S + 1, R) + part, BF16),
        vmem((S + 1, R) + part, BF16),
        vmem((S, R * B, K * B), BF16),
        vmem((K * B, HF), BF16),
        vmem((R * B, HF), F32),
        vmem((2, R) + part, BF16),
        vmem((2, R) + part, BF16),
        vmem((2,) + part, F32),
        vmem(block, BF16),
        vmem((R,) + part, BF16),
        vmem((R,) + part, BF16),
        vmem((2, S, R) + part, BF16),
        vmem((2, X, R) + part, BF16),
        vmem((2, X, R) + part, BF16),
        vmem((2, X, R) + part, BF16),
        vmem((2, Z) + part, BF16),
        vmem((2, Z) + part, BF16),
        vmem((2, Z) + part, BF16),
        vmem((2, Z) + part, BF16),
        vmem((F, F), F32),
        vmem((F, F), F32),
        vmem((F // 2, F), F32),
        vmem((F // 2, F), F32),
        vmem((X, F // 2 // X, F), F32),
        vmem((F // 2 // X, F), F32),
        vmem((Y, F // 2 // X // Y, F), F32),
        vmem((F // 2 // X // Y, F), F32),
        vmem((Z, F // 2 // X // Y, F), F32),
        vmem((F, F), BF16),
        vmem(block, BF16),
        pltpu.SMEM((K, S), jnp.int32),
        pltpu.SMEM((K, S), jnp.int32),
        pltpu.SMEM((S,), jnp.int32),
        vmem((S * K, B, B), BF16),
        vmem(part, F32),
        pltpu.SemaphoreType.DMA((sems,)),
        pltpu.SemaphoreType.DMA((sems,)),
        pltpu.SemaphoreType.DMA((8,)),
    ]
    in_vmem = pl.BlockSpec(memory_space=pltpu.VMEM)
    in_hbm = pl.BlockSpec(memory_space=pltpu.HBM)
    return pl.pallas_call(
        functools.partial(layer_kernel, dims),
        out_shape=(
            jax.ShapeDtypeStruct(block, BF16),
            jax.ShapeDtypeStruct((F, F), F32),
            jax.ShapeDtypeStruct(block, BF16),
        ),
        in_specs=[in_hbm] * 7,
        out_specs=(in_vmem, in_vmem, in_vmem),
        scratch_shapes=scratch,
        compiler_params=pltpu.CompilerParams(
            collective_id=0, has_side_effects=True, vmem_limit_bytes=63 << 20
        ),
        name="layer",
    )(
        features,
        weight,
        cotangent,
        tile_row[0, 0].T,
        tile_col[0, 0].T,
        tile_count[0, 0],
        tile_vals.reshape((S * K, B, B)),
    )


def solution(mesh):
    return jax.shard_map(
        on_device,
        mesh=mesh,
        in_specs=(
            P(("rep", "blk"), None),
            P(),
            P(("rep", "blk"), None),
            P("rep", "blk", None, None),
            P("rep", "blk", None, None),
            P("rep", "blk", None),
            P("rep", "blk", None, None, None, None),
        ),
        out_specs=(P(("rep", "blk"), None), P(), P(("rep", "blk"), None)),
        check_vma=False,
    )
```

time: 175 us -> 155 us (0.89)
  Pallas kernels: 168 us -> 147 us
    pallas_call x1, Pallas kernels: 168 us -> 147 us  [on_device(): pl.pallas_call(functools.partial(layer_kernel, dims), out_shape=(jax.Shap...]
where the time goes in v3:
time: 155 us; the launch traced here: 152 us
  Pallas kernels  147 us (95%)
  local copies, waits for them, and re-layouts  3.81 us (2%)
    pallas_call x1, Pallas kernels, on_device(): pl.pallas_call(functools.partial(layer_kernel, dims), out_shape=(jax.Shap...  147 us
    unnamed x5, local copies, waits for them, and re-layouts  3.81 us

profile of v3, /device:TPU:1, one launch (start us, length us, event | category | flops | bytes accessed | tf_op | source)
XLA Modules:
  0.0 151.5 jit_solution(12129911367017465790)
XLA Ops:
  0.6 147.1 %layer.1 = (bf16[128,256]{1,0:T(8,128)(2,1)}, f32[256,256]{1,0:T(8,128)}, bf16[128,256]{1,0:T(8,128)(2,1)}) custom-call(bf16[128,256]{1,0:T(8,128)(2,1)} %feat_hbm.1, bf16[256,256]{1,0:T(8,128)(2,1)} %weight_hbm.1, bf16[128,256]{1,0:T(8,128)(2,1)} %cot_hbm.1, s32[4,8]{1,0:T(4,128)} %bitcast.9, s32[4,8]{1,0:T(4,128)} %bitcast.10, s32[8]{0:T(128)} %bitcast.11, ...), custom_call_target="tpu_custom_call" | custom-call | tf_op jit(solution)/shard_map/layer/pallas_call | solution.py:602
  147.7 1.5 copy.13
  149.2 0.0 copy-start
  149.2 1.7 %copy.14 = f32[256,256]{1,0:T(8,128)} copy(f32[256,256]{1,0:T(8,128)} %get-tuple-element.7) | data formatting | bytes 524288
  150.9 0.0 copy-done
  150.9 0.6 copy.15
Async XLA Ops:
  149.2 1.7 %copy-start = (bf16[128,256]{1,0:T(8,128)(2,1)S(1)}, bf16[128,256]{1,0:T(8,128)(2,1)}, u32[]{:S(2)}) copy-start(bf16[128,256]{1,0:T(8,128)(2,1)} %get-tuple-element.8) | copy-start | bytes 196612

commit v4 on v3

--- a/solution.py
+++ b/solution.py
@@ -11,6 +11,7 @@
 BF16 = jnp.bfloat16
 LATE = 2.5
 BLATE = 2.5
+TAIL = True
 F32 = jnp.float32
 MESH = pl.DeviceIdType.MESH
 
@@ -97,15 +98,18 @@
         used[0] += n
         return used[0] - n
 
-    def copy(src, dst, i, dev):
+    def copy(src, dst, i, dev, out=None):
         return pltpu.make_async_remote_copy(
             src_ref=src,
             dst_ref=dst,
-            send_sem=send.at[i],
+            send_sem=send.at[i if out is None else out],
             recv_sem=recv.at[i],
             device_id=dev,
             device_id_type=MESH,
         )
+
+    def left(like, i):
+        copy(like, like, i, sib).wait_send()
 
     def arrived(dst, i):
         copy(dst, dst, i, sib).wait_recv()
@@ -177,10 +181,13 @@
             arrived(block, qz + number[e])
         for k in children(e)[::-1]:
             hop = k[0] * (k[1] - e[1])
-            go(copy(block, block, qz + number[k], z_dev(hop)))
+            copy(block, block, qz + number[k], z_dev(hop), qz).start()
+
+    def f_to(half):
+        return ((2 * y + half + (zh + r + half) % 2 + r - zh + R) % R) // 2
 
     def f_y_to(e):
-        return ((2 * y + slot_of(e) // R + role_of(e) + r - zh + R) % R) // 2
+        return f_to(slot_of(e) // R)
 
     def f_y_block(h, e):
         w = role_of(e)
@@ -197,12 +204,8 @@
 
         @pl.when(to != y)
         def _():
-            copy(zbuf.at[h, slot], f_y_block(h, e), i, at(to, z, x, c)).start()
-
-    def f_y_sent(h, e):
-        @pl.when(f_y_to(e) != y)
-        def _():
-            copy(zbuf.at[h, 0], zbuf.at[h, 0], fq[h][1] + number[e], sib).wait_send()
+            out = fq[h][1] + slot // R
+            copy(zbuf.at[h, slot], f_y_block(h, e), i, at(to, z, x, c), out).start()
 
     def f_x(h, e):
         w, b = role_of(e), slot_of(e) % R
@@ -213,7 +216,8 @@
 
             @pl.when((x < (x + d) % X) == (w == 0))
             def _():
-                copy(src, feats[h].at[s, b], qx + d * R + b, x_dev(d)).start()
+                i = qx + d * R
+                copy(src, feats[h].at[s, b], i + b, x_dev(d), i).start()
 
         @pl.when(w == c)
         def _():
@@ -275,20 +279,25 @@
         for d in range(1, R):
             rd = (r + d) % R
             accb[h, d] = acc[pl.ds(pl.multiple_of(rd * B, B), B), :].astype(BF16)
-            go(copy(accb.at[h, d], rsin.at[h, d], rq[h] + d, at(y, zh * R + rd, x, c)))
+            dev = at(y, zh * R + rd, x, c)
+            copy(accb.at[h, d], rsin.at[h, d], rq[h] + d, dev, rq[h]).start()
         rsown[h] = acc[own_rows, :]
 
     def f_sent(h):
-        _, _, qx, qs = fq[h]
+        qz, qy, qx, qs = fq[h]
+        panel = feats[h].at[0]
+        left(zbuf.at[h, pl.ds(0, Z - 1)], qz)
+        for half in range(2):
+
+            @pl.when(f_to(half) != y)
+            def _():
+                left(panel, qy + half)
+
         for d in range(X):
-            copy(feats[h].at[0], feats[h].at[0], qs + d, sib).wait_send()
-        for d in range(1, X):
-            for b in range(R):
-                copy(
-                    feats[h].at[0, b], feats[h].at[0, b], qx + d * R + b, sib
-                ).wait_send()
-        for e in order:
-            f_y_sent(h, e)
+            left(panel, qs + d)
+        for d in range(1, X):
+            left(panel, qx + d * R)
+        left(accb.at[h, pl.ds(1, R - 1)], rq[h])
 
     events = []
     top = len(levels)
@@ -337,7 +346,7 @@
         for d in range(1, R):
             rd = (r + d) % R
             mine = gpanel[h].at[r]
-            go(copy(mine, mine, gq[h] + d, at(y, zh * R + rd, x, c)))
+            copy(mine, mine, gq[h] + d, at(y, zh * R + rd, x, c), gq[h]).start()
     act_ref[...] = (preact * sig).astype(BF16)
     w_own[...] = lax.dot_general(
         agg, slope, (((0,), (0,)), ((), ())), preferred_element_type=F32
@@ -352,6 +361,8 @@
     qw = slots(1)
     go(copy(w_own.at[w_rows(1 - c, half_rows)], w_sib, qw, sib))
     masked_tiles(col_ref, True)
+    for h in range(2):
+        f_sent(h)
     arrived(w_sib, qw)
     w_half[...] = w_own[w_rows(c, half_rows), :] + w_sib[...]
     qw = slots(X)
@@ -395,11 +406,14 @@
                 xout[h, d, b] = (
                     cbuf[h, 2 * xd + c, b].astype(F32) + sibin[h, d, b].astype(F32)
                 ).astype(BF16)
-                i = bq[h][1] + d * R + b
-                copy(xout.at[h, d, b], xin.at[h, d, b], i, x_dev(d)).start()
+                i = bq[h][1] + d * R
+                copy(xout.at[h, d, b], xin.at[h, d, b], i + b, x_dev(d), i).start()
+
+    def b_to(half):
+        return ((2 * y + zh - r - (zh + r + half) % 2 + 2 * R) % R) // 2
 
     def b_y_to(e):
-        return ((2 * y + zh - r - role_of(e) + 2 * R) % R) // 2
+        return b_to(slot_of(e) // R)
 
     def b_y(h, e):
         w, b, i = role_of(e), slot_of(e) % R, bq[h][2] + number[e]
@@ -423,12 +437,7 @@
 
         @pl.when(to != y)
         def _():
-            copy(src, dst, i, at(to, z, x, c)).start()
-
-    def b_y_sent(h, e):
-        @pl.when(b_y_to(e) != y)
-        def _():
-            copy(yout.at[h, 0], yout.at[h, 0], bq[h][2] + number[e], sib).wait_send()
+            copy(src, dst, i, at(to, z, x, c), bq[h][2] + slot_of(e) // R).start()
 
     def b_z(h, e):
         g, m = e
@@ -442,7 +451,8 @@
             fgrad_ref[:, h * HF : (h + 1) * HF] = val.astype(BF16)
         else:
             zout[h, n] = val.astype(BF16)
-            go(copy(zout.at[h, n], zin.at[h, n], qz + n, z_dev(-g * (2 - m % 2))))
+            dev = z_dev(-g * (2 - m % 2))
+            copy(zout.at[h, n], zin.at[h, n], qz + n, dev, qz).start()
 
     def w_piece(c_, x_, y_):
         at_row = c_ * half_rows + x_ * x_rows
@@ -528,19 +538,28 @@
     wgrad_ref[...] = w_full[...]
 
     for h in range(2):
-        f_sent(h)
-        qs, qx, _, _ = bq[h]
+        qs, qx, qy, qz = bq[h]
+        panel = cbuf.at[h, 0]
+        left(accb.at[h, pl.ds(1, R - 1)], gq[h])
         for d in range(X):
-            copy(cbuf.at[h, 0], cbuf.at[h, 0], qs + d, sib).wait_send()
-        for d in range(1, X):
-            for b in range(R):
-                copy(
-                    xout.at[h, d, b], xout.at[h, d, b], qx + d * R + b, sib
-                ).wait_send()
-        for e in order:
-            b_y_sent(h, e)
+            left(panel, qs + d)
+        for d in range(1, X):
+            left(panel, qx + d * R)
+        for half in range(2):
+
+            @pl.when(b_to(half) != y)
+            def _():
+                left(panel, qy + half)
+
+        left(zout.at[h, pl.ds(0, Z - 1)], qz)
     for cp in sent:
         cp.wait_send()
+
+
+def result_kernel(*refs):
+    half = len(refs) // 2
+    for src, dst in zip(refs[:half], refs[half:]):
+        dst[...] = src[...]
 
 
 def on_device(features, weight, cotangent, tile_row, tile_col, tile_count, tile_vals):
@@ -599,7 +618,7 @@
     ]
     in_vmem = pl.BlockSpec(memory_space=pltpu.VMEM)
     in_hbm = pl.BlockSpec(memory_space=pltpu.HBM)
-    return pl.pallas_call(
+    results = pl.pallas_call(
         functools.partial(layer_kernel, dims),
         out_shape=(
             jax.ShapeDtypeStruct(block, BF16),
@@ -622,6 +641,15 @@
         tile_count[0, 0],
         tile_vals.reshape((S * K, B, B)),
     )
+    if not TAIL:
+        return results
+    return pl.pallas_call(
+        result_kernel,
+        out_shape=tuple(jax.ShapeDtypeStruct(v.shape, v.dtype) for v in results),
+        in_specs=[in_vmem] * 3,
+        out_specs=(in_vmem,) * 3,
+        name="results",
+    )(*results)
 
 
 def solution(mesh):

time: 155 us -> 149 us (0.961)
  the two profiles are of different devices: /device:TPU:1 before, /device:TPU:2 now
where the time goes in v4:
time: 149 us
  Pallas kernels  148 us (99%)
    pallas_call x1, Pallas kernels, on_device(): pl.pallas_call(functools.partial(layer_kernel, dims), out_shape=(jax.Shap...  147 us

profile of v4, /device:TPU:2, one launch (start us, length us, event | category | flops | bytes accessed | tf_op | source)
XLA Modules:
  0.0 149.0 jit_solution(1773392483466567819)
XLA Ops:
  0.6 146.6 %layer.1 = (bf16[128,256]{1,0:T(8,128)(2,1)}, f32[256,256]{1,0:T(8,128)}, bf16[128,256]{1,0:T(8,128)(2,1)}) custom-call(bf16[128,256]{1,0:T(8,128)(2,1)} %feat_hbm.1, bf16[256,256]{1,0:T(8,128)(2,1)} %weight_hbm.1, bf16[128,256]{1,0:T(8,128)(2,1)} %cot_hbm.1, s32[4,8]{1,0:T(4,128)} %bitcast.9, s32[4,8]{1,0:T(4,128)} %bitcast.10, s32[8]{0:T(128)} %bitcast.11, ...), custom_call_target="tpu_custom_call" | custom-call | tf_op jit(solution)/shard_map/layer/pallas_call | solution.py:621
  147.3 1.7 %results.1 = (bf16[128,256]{1,0:T(8,128)(2,1)}, f32[256,256]{1,0:T(8,128)}, bf16[128,256]{1,0:T(8,128)(2,1)}) custom-call(bf16[128,256]{1,0:T(8,128)(2,1)} %get-tuple-element.6.refs_0_, f32[256,256]{1,0:T(8,128)} %get-tuple-element.7.refs_1_, bf16[128,256]{1,0:T(8,128)(2,1)} %get-tuple-element.8.refs_2_), custom_call_target="tpu_custom_call" | custom-call | tf_op jit(solution)/shard_map/results/pallas_call | solution.py:646

commit v5 on v4

--- a/solution.py
+++ b/solution.py
@@ -269,6 +269,7 @@
         lax.fori_loop(0, S, step, 0)
 
     rq = [slots(R), slots(R)]
+    near_first = sorted(range(1, R), key=lambda d: min(d, R - d))
     own_rows = pl.ds(pl.multiple_of(r * B, B), B)
 
     def f_finish(h):
@@ -276,7 +277,7 @@
         for d in range(X):
             arrived(feats[h].at[2 * ((x - d + X) % X) + 1 - c], qs + d)
         forward_products(h)
-        for d in range(1, R):
+        for d in near_first:
             rd = (r + d) % R
             accb[h, d] = acc[pl.ds(pl.multiple_of(rd * B, B), B), :].astype(BF16)
             dev = at(y, zh * R + rd, x, c)
@@ -343,7 +344,7 @@
     gq = [slots(R), slots(R)]
     for h in range(2):
         gpanel[h][r] = back[:, h * HF : (h + 1) * HF].astype(BF16)
-        for d in range(1, R):
+        for d in near_first:
             rd = (r + d) % R
             mine = gpanel[h].at[r]
             copy(mine, mine, gq[h] + d, at(y, zh * R + rd, x, c), gq[h]).start()

time: 149 us -> 149 us (level)
  the two profiles are of different devices: /device:TPU:2 before, /device:TPU:1 now
where the time goes in v5:
time: 149 us
  Pallas kernels  148 us (99%)
    pallas_call x1, Pallas kernels, on_device(): pl.pallas_call(functools.partial(layer_kernel, dims), out_shape=(jax.Shap...  147 us

profile of v5, /device:TPU:1, one launch (start us, length us, event | category | flops | bytes accessed | tf_op | source)
XLA Modules:
  0.0 148.9 jit_solution(7882133739409692972)
XLA Ops:
  0.6 146.5 %layer.1 = (bf16[128,256]{1,0:T(8,128)(2,1)}, f32[256,256]{1,0:T(8,128)}, bf16[128,256]{1,0:T(8,128)(2,1)}) custom-call(bf16[128,256]{1,0:T(8,128)(2,1)} %feat_hbm.1, bf16[256,256]{1,0:T(8,128)(2,1)} %weight_hbm.1, bf16[128,256]{1,0:T(8,128)(2,1)} %cot_hbm.1, s32[4,8]{1,0:T(4,128)} %bitcast.9, s32[4,8]{1,0:T(4,128)} %bitcast.10, s32[8]{0:T(128)} %bitcast.11, ...), custom_call_target="tpu_custom_call" | custom-call | tf_op jit(solution)/shard_map/layer/pallas_call | solution.py:622
  147.1 1.7 %results.1 = (bf16[128,256]{1,0:T(8,128)(2,1)}, f32[256,256]{1,0:T(8,128)}, bf16[128,256]{1,0:T(8,128)(2,1)}) custom-call(bf16[128,256]{1,0:T(8,128)(2,1)} %get-tuple-element.6.refs_0_, f32[256,256]{1,0:T(8,128)} %get-tuple-element.7.refs_1_, bf16[128,256]{1,0:T(8,128)(2,1)} %get-tuple-element.8.refs_2_), custom_call_target="tpu_custom_call" | custom-call | tf_op jit(solution)/shard_map/results/pallas_call | solution.py:647
